TPU v7x, 256 devices: a whole 4x4x8 slice. The times are simulated.
256 devices in a mesh: rows: 32 (over z, y), irrep: 8 (over x, core).
Axes of the slice: x: 4, y: 4, z: 8, core: 2. Of those that a mesh axis runs over, the one named last changes fastest.
Arguments:
- coefficients: float32 [8, 2560, 2560], P('irrep', 'rows'), may hold values from -6 to 6
- block_codes: int32 [8, 4, 4, 320], P('irrep'), may hold values from -1 to 19, as said below
- tile_bank: float32 [8, 4, 8, 128, 128], P('irrep'), may hold values from -0.125 to 0.125
Outputs:
- sigma_vector: float32 [8, 2560, 2560], P('irrep', 'rows')
Inputs may be any that keep to these rules, and one draw needn't show every extreme that they name: Fields 0 and 1 of block_codes[g, k] are block numbers below 20 for k = 0, 3 and below 20 for k = 1, 2; the first of them list the diagonal blocks 0, 1, ... in order, so every block row holds a listed block; field 2 is a tile number below 8; field 3 is -1 or +1.
All inputs are finite; a program needn't handle non-finite values.
Results may differ from a plain program's by a relative error of at most 0.0001.
Values sent between devices are 32-bit elements; how exact they have to be, the bound alone decides.
No kernel may reach another device: no remote copies, remote signals or barrier semaphores. Data moves between devices by JAX's collectives and lax.ppermute only.
A program may use at most 128 MiB of HBM per device.

v0:
```python
import functools

import jax
import jax.numpy as jnp
from jax import lax
from jax.experimental import pallas as pl
from jax.experimental.pallas import tpu as pltpu
from jax.sharding import PartitionSpec as P

LANES = 128
PACKED = 56
GROUP = 8
f32, bf16 = jnp.float32, jnp.bfloat16
VMEM, SMEM = pltpu.VMEM, pltpu.SMEM


def lane_of(rows):
    return lax.broadcasted_iota(jnp.int32, (rows, LANES), 1)


def rolled(value, shift):
    shift %= LANES
    return value if shift == 0 else pltpu.roll(value, shift, 1)


def pack(z):
    by32, by64, by80 = rolled(z[48:64], 32), rolled(z[64:80], 64), rolled(z[48:80], 80)
    top = jnp.where(lane_of(32) < 80, z[0:32], by80)
    middle = jnp.where(lane_of(16) < 80, z[32:48], jnp.where(lane_of(16) < 112, by32, by64))
    bottom = jnp.where(lane_of(8) < 16, by64[0:8], by80[24:32])
    return jnp.concatenate([top, middle, bottom], axis=0)


def unpack(p):
    by48 = rolled(p[0:32], 48)
    rows48 = jnp.where(lane_of(16) < 48, by48[0:16], rolled(p[32:48], 96))
    tail = rolled(p[32:48], 64)
    lane = lane_of(8)
    rows64 = jnp.where(lane < 48, by48[16:24], jnp.where(lane < 64, tail[0:8], rolled(p[48:56], 64)))
    rows72 = jnp.where(lane < 48, by48[24:32], jnp.where(lane < 64, tail[8:16], rolled(p[48:56], 48)))
    return jnp.concatenate([p[0:48], rows48, rows64, rows72], axis=0)


def send_transposed(tile_at, count, send_ref, turned_ref):
    rows = turned_ref.shape[0] // send_ref.shape[0]

    def turn(j, _):
        turned_ref[pl.ds(pl.multiple_of(j * LANES, LANES), LANES), 0:rows] = tile_at(j).T
        return 0

    lax.fori_loop(0, count, turn, 0)

    def one(d, _):
        send_ref[d] = pack(turned_ref[pl.ds(pl.multiple_of(d * rows, 8), rows), :])
        return 0

    lax.fori_loop(0, send_ref.shape[0], one, 0)


def split_into(lhs_ref, j, value):
    rows = value.shape[0]
    high = value.astype(bf16)
    low = (value - high.astype(f32)).astype(bf16)
    at = pl.ds(pl.multiple_of(j * rows, 16), rows)
    lhs_ref[at, 0:128] = high
    lhs_ref[at, 128:256] = low
    lhs_ref[at, 256:384] = high


def receive_rows(recv_ref, pieces_ref, lhs_ref):
    rows = pieces_ref.shape[1]

    def group(g, _):
        for c in range(GROUP):
            pieces_ref[c] = unpack(recv_ref[g * GROUP + c])
        for b in range(GROUP * rows // LANES):
            first, last = b * LANES // rows, (b * LANES + LANES - 1) // rows
            value = rolled(pieces_ref[last], last * rows - b * LANES)
            for c in range(last - 1, first - 1, -1):
                end = c * rows + rows - b * LANES
                value = jnp.where(
                    lane_of(rows) < end, rolled(pieces_ref[c], c * rows - b * LANES), value
                )
            split_into(lhs_ref, g * (GROUP * rows // LANES) + b, value)
        return 0

    lax.fori_loop(0, recv_ref.shape[0] // GROUP, group, 0)


def send_rows(sum_ref, send_ref):
    rows = sum_ref.shape[1]

    def group(g, _):
        base = g * (GROUP * rows // LANES)
        for c in range(GROUP):
            b, o = c * rows // LANES, c * rows % LANES
            value = rolled(sum_ref[base + b], -o)
            if o + rows > LANES:
                value = jnp.where(
                    lane_of(rows) < LANES - o, value, rolled(sum_ref[base + b + 1], -o)
                )
            send_ref[g * GROUP + c] = pack(value)
        return 0

    lax.fori_loop(0, send_ref.shape[0] // GROUP, group, 0)


def operate(which_op, codes_ref, weights_ref, lhs_ref, products_ref, sum_ref):
    rows = sum_ref.shape[1]
    wide = 2 * LANES

    def multiply(n, _):
        at = pl.ds(pl.multiple_of(n * wide, wide), wide)
        products_ref[:, at] = jnp.dot(
            lhs_ref[...], weights_ref[:, at], preferred_element_type=f32
        )
        return 0

    lax.fori_loop(0, weights_ref.shape[1] // wide, multiply, 0)

    def add(m, _):
        i, j = codes_ref[which_op, 0, m], codes_ref[which_op, 1, m]
        t, sign = codes_ref[which_op, 2, m], codes_ref[which_op, 3, m].astype(f32)
        product = products_ref[
            pl.ds(pl.multiple_of(j * rows, 8), rows), pl.ds(pl.multiple_of(t * LANES, LANES), LANES)
        ]
        sum_ref[i] += sign * product
        return 0

    lax.fori_loop(0, codes_ref.shape[2], add, 0, unroll=8)


def columns(ref, j):
    return ref[:, pl.ds(pl.multiple_of(j * LANES, LANES), LANES)]


def format_kernel(c_ref, send_ref, turned_ref):
    send_transposed(lambda j: columns(c_ref, j), c_ref.shape[1] // LANES, send_ref, turned_ref)


def weights_kernel(tiles_ref, weights_ref):
    def one(at, _):
        k, t = at // tiles_ref.shape[1], at % tiles_ref.shape[1]
        tile = tiles_ref[k, t].T
        high = tile.astype(bf16)
        low = (tile - high.astype(f32)).astype(bf16)
        lanes = pl.ds(pl.multiple_of(t * LANES, LANES), LANES)
        weights_ref[k, 0:128, lanes] = high
        weights_ref[k, 128:256, lanes] = high
        weights_ref[k, 256:384, lanes] = low
        return 0

    lax.fori_loop(0, tiles_ref.shape[0] * tiles_ref.shape[1], one, 0)


def split_all(c_ref, lhs_ref):
    def one(j, _):
        split_into(lhs_ref, j, columns(c_ref, j))
        return 0

    lax.fori_loop(0, c_ref.shape[1] // LANES, one, 0)


def beta_kernel(codes_ref, c_ref, weights_ref, sum_ref, lhs_ref, products_ref):
    split_all(c_ref, lhs_ref)
    sum_ref[...] = jnp.zeros_like(sum_ref)
    operate(0, codes_ref, weights_ref, lhs_ref, products_ref, sum_ref)


def mixed_kernel(codes_ref, c_ref, weights_ref, send_ref, lhs_ref, products_ref, sum_ref, turned_ref):
    split_all(c_ref, lhs_ref)
    sum_ref[...] = jnp.zeros_like(sum_ref)
    operate(3, codes_ref, weights_ref, lhs_ref, products_ref, sum_ref)
    send_transposed(lambda j: sum_ref[j], sum_ref.shape[0], send_ref, turned_ref)


def alpha_kernel(codes_ref, recv_ref, weights_ref, sum_ref, lhs_ref, products_ref, pieces_ref):
    receive_rows(recv_ref, pieces_ref, lhs_ref)
    sum_ref[...] = jnp.zeros_like(sum_ref)
    operate(1, codes_ref, weights_ref, lhs_ref, products_ref, sum_ref)


def cross_kernel(codes_ref, recv_ref, weights_ref, own_ref, send_ref, lhs_ref, products_ref, pieces_ref, sum_ref):
    receive_rows(recv_ref, pieces_ref, lhs_ref)
    sum_ref[...] = own_ref[...]
    operate(2, codes_ref, weights_ref, lhs_ref, products_ref, sum_ref)
    send_rows(sum_ref, send_ref)


def final_kernel(recv_ref, beta_ref, out_ref, turned_ref):
    rows = out_ref.shape[0]

    def one(d, _):
        turned_ref[pl.ds(pl.multiple_of(d * rows, 8), rows), :] = unpack(recv_ref[d])
        return 0

    lax.fori_loop(0, recv_ref.shape[0], one, 0)

    def turn(j, _):
        back = turned_ref[pl.ds(pl.multiple_of(j * LANES, LANES), LANES), :].T
        out_ref[:, pl.ds(pl.multiple_of(j * LANES, LANES), LANES)] = back[0:rows] + beta_ref[j]
        return 0

    lax.fori_loop(0, beta_ref.shape[0], turn, 0)


def call(kernel, out, scratch, operands, flops, name):
    specs = [
        pl.BlockSpec(memory_space=SMEM if x.dtype == jnp.int32 else VMEM) for x in operands
    ]
    moved = sum(x.size * x.dtype.itemsize for x in operands)
    return pl.pallas_call(
        kernel,
        out_shape=out,
        in_specs=specs,
        out_specs=pl.BlockSpec(memory_space=VMEM),
        scratch_shapes=scratch,
        compiler_params=pltpu.CompilerParams(vmem_limit_bytes=40 << 20),
        cost_estimate=pl.CostEstimate(flops=flops, bytes_accessed=moved, transcendentals=0),
        name=name,
    )(*operands)


def body(coefficients, block_codes, tile_bank):
    shards = lax.axis_size("rows")
    irreps = lax.axis_size("irrep")
    own, codes, tiles = coefficients[0], block_codes[0], tile_bank[0]
    rows, width = own.shape
    blocks, tile_count = width // LANES, tiles.shape[1]
    flops = 6 * rows * blocks * LANES * LANES * tile_count

    packed = jax.ShapeDtypeStruct((shards, PACKED, LANES), f32)
    summed = jax.ShapeDtypeStruct((blocks, rows, LANES), f32)
    lhs = VMEM((blocks * rows, 3 * LANES), bf16)
    products = VMEM((blocks * rows, tile_count * LANES), f32)
    turned = VMEM((width, LANES), f32)
    pieces = VMEM((GROUP, rows, LANES), f32)
    total = VMEM((blocks, rows, LANES), f32)

    def exchange(x):
        return lax.all_to_all(x, "rows", split_axis=0, concat_axis=0, tiled=True)

    partner = lax.ppermute(own, "irrep", [(i, i ^ irreps // 2) for i in range(irreps)])
    columns_in = exchange(call(format_kernel, packed, [turned], (own,), 1 << 20, "format"))
    weights = call(
        weights_kernel,
        jax.ShapeDtypeStruct((tiles.shape[0], 3 * LANES, tile_count * LANES), bf16),
        [],
        (tiles,),
        1 << 20,
        "weights",
    )
    mixed = call(
        mixed_kernel, packed, [lhs, products, total, turned], (codes, partner, weights[3]), flops, "mixed"
    )
    cross_in = exchange(mixed)
    beta = call(beta_kernel, summed, [lhs, products], (codes, own, weights[0]), flops, "beta")
    alpha = call(
        alpha_kernel, summed, [lhs, products, pieces], (codes, columns_in, weights[1]), flops, "alpha"
    )
    returned = exchange(
        call(
            cross_kernel,
            packed,
            [lhs, products, pieces, total],
            (codes, cross_in, weights[2], alpha),
            flops,
            "cross",
        )
    )
    out = call(
        final_kernel, jax.ShapeDtypeStruct((rows, width), f32), [turned], (returned, beta), 1 << 20, "final"
    )
    return out[None]


def solution(mesh):
    in_specs = (
        P("irrep", "rows", None),
        P("irrep", None, None, None),
        P("irrep", None, None, None, None),
    )
    out_specs = P("irrep", "rows", None)
    return jax.shard_map(body, mesh=mesh, in_specs=in_specs, out_specs=out_specs, check_vma=False)
```

profile of v0, /device:TPU:4, one launch (start us, length us, event | category | flops | bytes accessed | tf_op | source)
XLA Modules:
  0.0 132.5 jit_solution(15042673612576654605)
XLA Ops:
  0.0 0.0 copy-start
  0.0 0.0 copy-start.1
  0.0 1.3 copy-done.1
  1.3 5.4 %format.1 = f32[32,56,128]{2,1,0:T(8,128)} custom-call(f32[80,2560]{1,0:T(8,128)S(1)} %bitcast.14), custom_call_target="tpu_custom_call" | custom-call | flops 1048576 | bytes 819200 | tf_op jit(solution)/shard_map/format/pallas_call | solution.py:212
  6.7 11.5 %all-to-all-start.1 = ((f32[32,56,128]{2,1,0:T(8,128)}), f32[32,56,128]{2,1,0:T(8,128)S(1)}, u32[]{:S(2)}, u32[]{:S(2)}) async-start(f32[32,56,128]{2,1,0:T(8,128)} %format.1), calls=%async_computation.1 | async-start | bytes 1835008 | tf_op jit(solution)/shard_map/all_to_all | solution.py:241
  18.2 0.6 collective-permute-start
  18.8 0.0 copy-done
  18.8 3.3 %weights.1 = bf16[4,384,1024]{2,1,0:T(8,128)(2,1)S(1)} custom-call(f32[4,8,128,128]{3,2,1,0:T(8,128)S(1)} %bitcast.12), custom_call_target="tpu_custom_call" | custom-call | flops 1048576 | bytes 2097152 | tf_op jit(solution)/shard_map/weights/pallas_call | solution.py:212
  22.2 0.0 copy-start.4
  22.2 1.4 %slice_bitcast_fusion = (bf16[384,1024]{1,0:T(8,128)(2,1)S(1)}, bf16[384,1024]{1,0:T(8,128)(2,1)S(1)}, bf16[384,1024]{1,0:T(8,128)(2,1)}, bf16[384,1024]{1,0:T(8,128)(2,1)S(1)}) fusion(bf16[4,384,1024]{2,1,0:T(8,128)(2,1)S(1)} %weights.1), kind=kLoop, calls=%fused_computation | loop fusion | bytes 6291456 | tf_op jit(solution)/shard_map/squeeze | solution.py:257
  23.6 16.2 %collective-permute-done.c_ref = f32[80,2560]{1,0:T(8,128)S(1)} collective-permute-done((f32[80,2560]{1,0:T(8,128)}, f32[80,2560]{1,0:T(8,128)S(1)}, u32[]{:S(2)}, u32[]{:S(2)}) %collective-permute-start) | collective-permute-done | bytes 819232 | tf_op jit(solution)/shard_map/ppermute | solution.py:243
  39.7 0.0 copy-done.4
  39.7 11.9 %mixed.1 = f32[32,56,128]{2,1,0:T(8,128)} custom-call(s32[4,4,320]{2,1,0:T(4,128)S(1)} %bitcast.16, f32[80,2560]{1,0:T(8,128)S(1)} %collective-permute-done.c_ref, bf16[384,1024]{1,0:T(8,128)(2,1)S(1)} %get-tuple-element.8.weights_ref), custom_call_target="tpu_custom_call" | custom-call | flops 1258291200 | bytes 1626112 | tf_op jit(solution)/shard_map/mixed/pallas_call | solution.py:212
  51.7 0.0 all-to-all-done.1.recv_ref
  51.7 9.5 %all-to-all-start = ((f32[32,56,128]{2,1,0:T(8,128)}), f32[32,56,128]{2,1,0:T(8,128)S(1)}, u32[]{:S(2)}, u32[]{:S(2)}) async-start(f32[32,56,128]{2,1,0:T(8,128)} %mixed.1), calls=%async_computation | async-start | bytes 1835008 | tf_op jit(solution)/shard_map/all_to_all | solution.py:241
  61.2 7.2 %alpha.1.own_ref = f32[20,80,128]{2,1,0:T(8,128)S(1)} custom-call(s32[4,4,320]{2,1,0:T(4,128)S(1)} %bitcast.17, f32[32,56,128]{2,1,0:T(8,128)S(1)} %all-to-all-done.1.recv_ref, bf16[384,1024]{1,0:T(8,128)(2,1)S(1)} %get-tuple-element.6.weights_ref), custom_call_target="tpu_custom_call" | custom-call | flops 1258291200 | bytes 1724416 | tf_op jit(solution)/shard_map/alpha/pallas_call | solution.py:212
  68.4 0.0 copy-start.5
  68.4 0.9 copy-done.5
  69.3 15.9 %all-to-all-done.recv_ref = f32[32,56,128]{2,1,0:T(8,128)S(1)} async-done(((f32[32,56,128]{2,1,0:T(8,128)}), f32[32,56,128]{2,1,0:T(8,128)S(1)}, u32[]{:S(2)}, u32[]{:S(2)}) %all-to-all-start) | async-done | bytes 917536 | tf_op jit(solution)/shard_map/all_to_all | solution.py:241
  85.1 0.0 copy-start.3
  85.1 1.1 copy-done.3
  86.3 0.0 copy-start.6
  86.3 1.1 copy-done.6
  87.4 0.0 copy-start.2
  87.4 10.1 %cross.1 = f32[32,56,128]{2,1,0:T(8,128)} custom-call(s32[4,4,320]{2,1,0:T(4,128)S(1)} %bitcast.18, f32[32,56,128]{2,1,0:T(8,128)S(1)} %all-to-all-done.recv_ref, bf16[384,1024]{1,0:T(8,128)(2,1)S(1)} %copy-done.3, f32[20,80,128]{2,1,0:T(8,128)S(1)} %copy-done.6), custom_call_target="tpu_custom_call" | custom-call | flops 1258291200 | bytes 2543616 | tf_op jit(solution)/shard_map/cross/pallas_call | solution.py:212
  97.5 5.4 %all-to-all-start.2 = ((f32[32,56,128]{2,1,0:T(8,128)}), f32[32,56,128]{2,1,0:T(8,128)S(1)}, u32[]{:S(2)}, u32[]{:S(2)}) async-start(f32[32,56,128]{2,1,0:T(8,128)} %cross.1), calls=%async_computation.2 | async-start | bytes 1835008 | tf_op jit(solution)/shard_map/all_to_all | solution.py:241
  102.9 0.0 copy-done.2
  102.9 6.4 %beta.1.beta_ref = f32[20,80,128]{2,1,0:T(8,128)S(1)} custom-call(s32[4,4,320]{2,1,0:T(4,128)S(1)} %bitcast.19, f32[80,2560]{1,0:T(8,128)S(1)} %bitcast.15, bf16[384,1024]{1,0:T(8,128)(2,1)S(1)} %get-tuple-element.5.weights_ref), custom_call_target="tpu_custom_call" | custom-call | flops 1258291200 | bytes 1626112 | tf_op jit(solution)/shard_map/beta/pallas_call | solution.py:212
  109.3 18.0 %all-to-all-done.2.recv_ref = f32[32,56,128]{2,1,0:T(8,128)S(1)} async-done(((f32[32,56,128]{2,1,0:T(8,128)}), f32[32,56,128]{2,1,0:T(8,128)S(1)}, u32[]{:S(2)}, u32[]{:S(2)}) %all-to-all-start.2) | async-done | bytes 917536 | tf_op jit(solution)/shard_map/all_to_all | solution.py:241
  127.3 5.2 %final.1 = f32[80,2560]{1,0:T(8,128)} custom-call(f32[32,56,128]{2,1,0:T(8,128)S(1)} %all-to-all-done.2.recv_ref, f32[20,80,128]{2,1,0:T(8,128)S(1)} %beta.1.beta_ref), custom_call_target="tpu_custom_call" | custom-call | flops 1048576 | bytes 1736704 | tf_op jit(solution)/shard_map/final/pallas_call | solution.py:212
Async XLA Ops:
  0.0 18.8 %copy-start = (f32[1,4,8,128,128]{4,3,2,1,0:T(8,128)S(1)}, f32[1,4,8,128,128]{4,3,2,1,0:T(8,128)}, u32[]{:S(2)}) copy-start(f32[1,4,8,128,128]{4,3,2,1,0:T(8,128)} %param.5) | copy-start | bytes 6291460
  0.0 1.3 copy-start.1
  6.7 44.9 %all-to-all-start.1 = ((f32[32,56,128]{2,1,0:T(8,128)}), f32[32,56,128]{2,1,0:T(8,128)S(1)}, u32[]{:S(2)}, u32[]{:S(2)}) async-start(f32[32,56,128]{2,1,0:T(8,128)} %format.1), calls=%async_computation.1 | async-start | bytes 1835008 | tf_op jit(solution)/shard_map/all_to_all | solution.py:241
  18.2 21.5 %collective-permute-start = (f32[80,2560]{1,0:T(8,128)}, f32[80,2560]{1,0:T(8,128)S(1)}, u32[]{:S(2)}, u32[]{:S(2)}) collective-permute-start(f32[80,2560]{1,0:T(8,128)} %bitcast.13), channel_id=1, source_target_pairs={{0,4},{1,5},{2,6},{3,7},{4,0},{5,1},{6,2},{7,3},{8,12},{9,13},{10,... | collective-permute-start | bytes 2457608 | tf_op jit(solution)/shard_map/ppermute | solution.py:243
  22.2 17.6 %copy-start.4 = (s32[1,4,4,320]{3,2,1,0:T(4,128)S(1)}, s32[1,4,4,320]{3,2,1,0:T(4,128)}, u32[]{:S(2)}) copy-start(s32[1,4,4,320]{3,2,1,0:T(4,128)} %param.4) | copy-start | bytes 61444
  51.7 33.5 %all-to-all-start = ((f32[32,56,128]{2,1,0:T(8,128)}), f32[32,56,128]{2,1,0:T(8,128)S(1)}, u32[]{:S(2)}, u32[]{:S(2)}) async-start(f32[32,56,128]{2,1,0:T(8,128)} %mixed.1), calls=%async_computation | async-start | bytes 1835008 | tf_op jit(solution)/shard_map/all_to_all | solution.py:241
  68.4 0.9 copy-start.5
  85.1 1.1 copy-start.3
  86.3 1.1 copy-start.6
  87.4 15.5 %copy-start.2 = (f32[1,80,2560]{2,1,0:T(8,128)S(1)}, f32[1,80,2560]{2,1,0:T(8,128)}, u32[]{:S(2)}) copy-start(f32[1,80,2560]{2,1,0:T(8,128)} %param.3) | copy-start | bytes 2457604
  97.5 29.8 %all-to-all-start.2 = ((f32[32,56,128]{2,1,0:T(8,128)}), f32[32,56,128]{2,1,0:T(8,128)S(1)}, u32[]{:S(2)}, u32[]{:S(2)}) async-start(f32[32,56,128]{2,1,0:T(8,128)} %cross.1), calls=%async_computation.2 | async-start | bytes 1835008 | tf_op jit(solution)/shard_map/all_to_all | solution.py:241
where the time goes:
time: 133 us
  waiting for transfers between devices  50.1 us (38%)
  Pallas kernels  49.6 us (37%)
  starting transfers between devices  27 us (20%)
  local copies, waits for them, and re-layouts  5.83 us (4%)
    pallas_call x7, Pallas kernels, call(): pl.pallas_call(kernel, out_shape=out, in_specs=specs, out_specs=pl.BlockS...  49.6 us
    all_to_all x3, waiting for transfers between devices, exchange(): return lax.all_to_all(x, 'rows', split_axis=0, concat_axis=0, tiled=True)  33.9 us
    all_to_all x3, starting transfers between devices, exchange(): return lax.all_to_all(x, 'rows', split_axis=0, concat_axis=0, tiled=True)  26.4 us
    ppermute x1, waiting for transfers between devices, body(): lax.ppermute(own, 'irrep', [(i, i ^ irreps // 2) for i in range(irreps)])  16.2 us
    unnamed x14, local copies, waits for them, and re-layouts  4.47 us
  transfers between devices with their start and end apart: 4, of which 3 were waited for; matrix products, arithmetic and copies ran while one was open for 1% of the time, Pallas kernels for 22%

commit v1 on v0

v1 whole, which is shorter than its diff:
```python
import jax
import jax.numpy as jnp
from jax import lax
from jax.experimental import pallas as pl
from jax.experimental.pallas import tpu as pltpu
from jax.sharding import PartitionSpec as P


LANES = 128
PACKED = 56
GROUP = 8
RUN = 8
f32, bf16 = jnp.float32, jnp.bfloat16
VMEM, SMEM = pltpu.VMEM, pltpu.SMEM


def lane_of(rows):
    return lax.broadcasted_iota(jnp.int32, (rows, LANES), 1)


def rolled(value, shift):
    shift %= LANES
    return value if shift == 0 else pltpu.roll(value, shift, 1)


def pack(z):
    by32, by64, by80 = rolled(z[48:64], 32), rolled(z[64:80], 64), rolled(z[48:80], 80)
    top = jnp.where(lane_of(32) < 80, z[0:32], by80)
    middle = jnp.where(lane_of(16) < 80, z[32:48], jnp.where(lane_of(16) < 112, by32, by64))
    bottom = jnp.where(lane_of(8) < 16, by64[0:8], by80[24:32])
    return jnp.concatenate([top, middle, bottom], axis=0)


def unpack(p):
    by48 = rolled(p[0:32], 48)
    rows48 = jnp.where(lane_of(16) < 48, by48[0:16], rolled(p[32:48], 96))
    tail = rolled(p[32:48], 64)
    lane = lane_of(8)
    rows64 = jnp.where(lane < 48, by48[16:24], jnp.where(lane < 64, tail[0:8], rolled(p[48:56], 64)))
    rows72 = jnp.where(lane < 48, by48[24:32], jnp.where(lane < 64, tail[8:16], rolled(p[48:56], 48)))
    return jnp.concatenate([p[0:48], rows48, rows64, rows72], axis=0)


def send_transposed(tile_at, count, send_ref, turned_ref):
    rows = turned_ref.shape[0] // send_ref.shape[0]

    def turn(j, _):
        turned_ref[pl.ds(pl.multiple_of(j * LANES, LANES), LANES), 0:rows] = tile_at(j).T
        return 0

    lax.fori_loop(0, count, turn, 0, unroll=5)

    def one(d, _):
        send_ref[d] = pack(turned_ref[pl.ds(pl.multiple_of(d * rows, 8), rows), :])
        return 0

    lax.fori_loop(0, send_ref.shape[0], one, 0, unroll=4)


def split_into(lhs_ref, j, value):
    rows = value.shape[0]
    high = value.astype(bf16)
    low = (value - high.astype(f32)).astype(bf16)
    at = pl.ds(pl.multiple_of(j * rows, 16), rows)
    lhs_ref[at, 0:128] = high
    lhs_ref[at, 128:256] = low
    lhs_ref[at, 256:384] = high


def receive_rows(recv_ref, pieces_ref, lhs_ref):
    rows = pieces_ref.shape[1]

    def group(g, _):
        for c in range(GROUP):
            pieces_ref[c] = unpack(recv_ref[g * GROUP + c])
        for b in range(GROUP * rows // LANES):
            first, last = b * LANES // rows, (b * LANES + LANES - 1) // rows
            value = rolled(pieces_ref[last], last * rows - b * LANES)
            for c in range(last - 1, first - 1, -1):
                end = c * rows + rows - b * LANES
                value = jnp.where(
                    lane_of(rows) < end, rolled(pieces_ref[c], c * rows - b * LANES), value
                )
            split_into(lhs_ref, g * (GROUP * rows // LANES) + b, value)
        return 0

    lax.fori_loop(0, recv_ref.shape[0] // GROUP, group, 0)


def send_rows(sum_ref, send_ref):
    rows = sum_ref.shape[1]

    def group(g, _):
        base = g * (GROUP * rows // LANES)
        for c in range(GROUP):
            b, o = c * rows // LANES, c * rows % LANES
            value = rolled(sum_ref[base + b], -o)
            if o + rows > LANES:
                value = jnp.where(
                    lane_of(rows) < LANES - o, value, rolled(sum_ref[base + b + 1], -o)
                )
            send_ref[g * GROUP + c] = pack(value)
        return 0

    lax.fori_loop(0, send_ref.shape[0] // GROUP, group, 0)


def operate(which_op, words_ref, starts_ref, weights_ref, lhs_ref, products_ref, sum_ref, first):
    blocks, rows, _ = sum_ref.shape
    tile_count = products_ref.shape[0] // blocks

    def multiply(n, _):
        at = pl.ds(pl.multiple_of(n * 2 * LANES, 2 * LANES), 2 * LANES)
        both = jnp.dot(lhs_ref[...], weights_ref[:, at], preferred_element_type=f32)
        for j in range(blocks):
            for half in range(2):
                products_ref[j * tile_count + 2 * n + half] = both[
                    j * rows : (j + 1) * rows, half * LANES : (half + 1) * LANES
                ]
        return 0

    lax.fori_loop(0, tile_count // 2, multiply, 0)

    def output_block(i, _):
        def run(q, total):
            for u in range(RUN):
                word = words_ref[which_op, q * RUN + u]
                sign = ((word & 1) - ((word >> 1) & 1)).astype(f32)
                total = total + sign * products_ref[word >> 2]
            return total

        sum_ref[i] = lax.fori_loop(
            starts_ref[which_op, i], starts_ref[which_op, i + 1], run, first(i)
        )
        return 0

    lax.fori_loop(0, blocks, output_block, 0)


def runs_of(block_codes, blocks, tile_count):
    row, column, tile, sign = (block_codes[:, field] for field in range(4))
    words = (column * tile_count + tile) * 4 + jnp.where(sign > 0, 1, 2)
    listed = row.shape[1]
    slots = (listed + blocks * (RUN - 1) + 127) // 128 * 128
    at = jnp.arange(listed, dtype=jnp.int32)
    block = jnp.arange(blocks, dtype=jnp.int32)
    within = jnp.sum(
        (row[:, None, :] == row[:, :, None]) & (at[None, None, :] < at[None, :, None]),
        axis=2,
        dtype=jnp.int32,
    )
    counts = jnp.sum(row[:, None, :] == block[None, :, None], axis=2, dtype=jnp.int32)
    runs = (counts + RUN - 1) // RUN
    begin = jnp.sum(jnp.where(block[None, None, :] < row[:, :, None], runs[:, None, :], 0), axis=2)
    place = begin * RUN + within
    slot = jnp.arange(slots, dtype=jnp.int32)
    grouped = jnp.sum(
        jnp.where(place[:, None, :] == slot[None, :, None], words[:, None, :], 0), axis=2
    )
    bound = jnp.arange(blocks + 1, dtype=jnp.int32)
    starts = jnp.sum(jnp.where(block[None, None, :] < bound[None, :, None], runs[:, None, :], 0), axis=2)
    return grouped.astype(jnp.int32), starts.astype(jnp.int32)


def columns(ref, j):
    return ref[:, pl.ds(pl.multiple_of(j * LANES, LANES), LANES)]


def format_kernel(c_ref, send_ref, turned_ref):
    send_transposed(lambda j: columns(c_ref, j), c_ref.shape[1] // LANES, send_ref, turned_ref)


def weights_kernel(tiles_ref, *weights_refs):
    for k, weights_ref in enumerate(weights_refs):

        def one(t, _):
            tile = tiles_ref[k, t].T
            high = tile.astype(bf16)
            low = (tile - high.astype(f32)).astype(bf16)
            lanes = pl.ds(pl.multiple_of(t * LANES, LANES), LANES)
            weights_ref[0:128, lanes] = high
            weights_ref[128:256, lanes] = high
            weights_ref[256:384, lanes] = low
            return 0

        lax.fori_loop(0, tiles_ref.shape[1], one, 0, unroll=2)


def split_all(c_ref, lhs_ref):
    def one(j, _):
        split_into(lhs_ref, j, columns(c_ref, j))
        return 0

    lax.fori_loop(0, c_ref.shape[1] // LANES, one, 0, unroll=4)


def zeros_like_block(ref):
    return lambda i: jnp.zeros(ref.shape[1:], f32)


def beta_kernel(words_ref, starts_ref, c_ref, weights_ref, sum_ref, lhs_ref, products_ref):
    split_all(c_ref, lhs_ref)
    operate(0, words_ref, starts_ref, weights_ref, lhs_ref, products_ref, sum_ref, zeros_like_block(sum_ref))


def mixed_kernel(words_ref, starts_ref, c_ref, weights_ref, send_ref, lhs_ref, products_ref, sum_ref, turned_ref):
    split_all(c_ref, lhs_ref)
    operate(3, words_ref, starts_ref, weights_ref, lhs_ref, products_ref, sum_ref, zeros_like_block(sum_ref))
    send_transposed(lambda j: sum_ref[j], sum_ref.shape[0], send_ref, turned_ref)


def alpha_kernel(words_ref, starts_ref, recv_ref, weights_ref, sum_ref, lhs_ref, products_ref, pieces_ref):
    receive_rows(recv_ref, pieces_ref, lhs_ref)
    operate(1, words_ref, starts_ref, weights_ref, lhs_ref, products_ref, sum_ref, zeros_like_block(sum_ref))


def cross_kernel(
    words_ref, starts_ref, recv_ref, weights_ref, own_ref, send_ref, lhs_ref, products_ref, pieces_ref, sum_ref
):
    receive_rows(recv_ref, pieces_ref, lhs_ref)
    operate(2, words_ref, starts_ref, weights_ref, lhs_ref, products_ref, sum_ref, lambda i: own_ref[i])
    send_rows(sum_ref, send_ref)


def final_kernel(recv_ref, beta_ref, out_ref, turned_ref):
    rows = out_ref.shape[0]

    def one(d, _):
        turned_ref[pl.ds(pl.multiple_of(d * rows, 8), rows), :] = unpack(recv_ref[d])
        return 0

    lax.fori_loop(0, recv_ref.shape[0], one, 0, unroll=4)

    def turn(j, _):
        back = turned_ref[pl.ds(pl.multiple_of(j * LANES, LANES), LANES), :].T
        out_ref[:, pl.ds(pl.multiple_of(j * LANES, LANES), LANES)] = back[0:rows] + beta_ref[j]
        return 0

    lax.fori_loop(0, beta_ref.shape[0], turn, 0, unroll=5)


def call(kernel, out, scratch, operands, flops):
    specs = [
        pl.BlockSpec(memory_space=SMEM if x.dtype == jnp.int32 else VMEM) for x in operands
    ]
    moved = sum(x.size * x.dtype.itemsize for x in operands)
    return pl.pallas_call(
        kernel,
        out_shape=out,
        in_specs=specs,
        out_specs=jax.tree.map(lambda _: pl.BlockSpec(memory_space=VMEM), out),
        scratch_shapes=scratch,
        compiler_params=pltpu.CompilerParams(vmem_limit_bytes=20 << 20),
        cost_estimate=pl.CostEstimate(flops=flops, bytes_accessed=moved, transcendentals=0),
    )(*operands)


def steps(coefficients, block_codes, tile_bank):
    shards = lax.axis_size("rows")
    irreps = lax.axis_size("irrep")
    own, codes, tiles = coefficients[0], block_codes[0], tile_bank[0]
    rows, width = own.shape
    blocks, tile_count = width // LANES, tiles.shape[1]
    flops = 6 * rows * blocks * LANES * LANES * tile_count

    packed = jax.ShapeDtypeStruct((shards, PACKED, LANES), f32)
    summed = jax.ShapeDtypeStruct((blocks, rows, LANES), f32)
    lhs = VMEM((blocks * rows, 3 * LANES), bf16)
    products = VMEM((blocks * tile_count, rows, LANES), f32)
    turned = VMEM((width, LANES), f32)
    pieces = VMEM((GROUP, rows, LANES), f32)
    total = VMEM((blocks, rows, LANES), f32)
    weights = jax.ShapeDtypeStruct((3 * LANES, tile_count * LANES), bf16)

    def exchange(x):
        return lax.all_to_all(x, "rows", split_axis=0, concat_axis=0, tiled=True)

    partner = lax.ppermute(own, "irrep", [(i, i ^ irreps // 2) for i in range(irreps)])
    listed = runs_of(codes, blocks, tile_count)
    columns_in = exchange(call(format_kernel, packed, [turned], (own,), 1 << 20))
    w0, w1, w2, w3 = call(weights_kernel, [weights] * tiles.shape[0], [], (tiles,), 1 << 20)
    mixed = call(mixed_kernel, packed, [lhs, products, total, turned], (*listed, partner, w3), flops)
    cross_in = exchange(mixed)
    beta = call(beta_kernel, summed, [lhs, products], (*listed, own, w0), flops)
    alpha = call(alpha_kernel, summed, [lhs, products, pieces], (*listed, columns_in, w1), flops)
    cross = call(cross_kernel, packed, [lhs, products, pieces, total], (*listed, cross_in, w2, alpha), flops)
    returned = exchange(cross)
    out = call(final_kernel, jax.ShapeDtypeStruct((rows, width), f32), [turned], (returned, beta), 1 << 20)
    return out[None]


def solution(mesh):
    in_specs = (
        P("irrep", "rows", None),
        P("irrep", None, None, None),
        P("irrep", None, None, None, None),
    )
    out_specs = P("irrep", "rows", None)
    return jax.shard_map(steps, mesh=mesh, in_specs=in_specs, out_specs=out_specs, check_vma=False)
```

time: 133 us -> 123 us (0.925)
  Pallas kernels: 49.6 us -> 35.8 us
  other arithmetic: 0 us -> 1.94 us
    pallas_call x7, Pallas kernels: 49.6 us -> 35.8 us  [call(): pl.pallas_call(kernel, out_shape=out, in_specs=specs, out_specs=jax.tree....]
    unnamed x14 -> x26, local copies, waits for them, and re-layouts: 4.47 us -> 7.14 us
    ppermute x1, waiting for transfers between devices: 16.2 us -> 14.2 us  [steps(): lax.ppermute(own, 'irrep', [(i, i ^ irreps // 2) for i in range(irreps)])]
    all_to_all x3, waiting for transfers between devices: 33.9 us -> 35.8 us  [exchange(): return lax.all_to_all(x, 'rows', split_axis=0, concat_axis=0, tiled=True)]
    reduce_sum x0 -> x5, other arithmetic: none -> 1.85 us  [the longest x1 0.71 us: runs_of(): jnp.sum((row[:, None, :] == row[:, :, None]) & (at[None, None, :] < at[No...]
    squeeze x1 -> x0, local copies, waits for them, and re-layouts: 1.36 us -> none  [body(): weights[0]]
  transfers between devices with their start and end apart: 4 -> 4, of which waited for: 3 -> 3; matrix products, arithmetic and copies ran while one was open for 1% -> 2% of each run, Pallas kernels for 22% -> 18%
where the time goes in v1:
time: 123 us; the launch traced here: 122 us
  waiting for transfers between devices  49.9 us (41%)
  Pallas kernels  35.8 us (29%)
  starting transfers between devices  27.1 us (22%)
  local copies, waits for them, and re-layouts  7.14 us (6%)
  other arithmetic  1.94 us (2%)
    all_to_all x3, waiting for transfers between devices, exchange(): return lax.all_to_all(x, 'rows', split_axis=0, concat_axis=0, tiled=True)  35.8 us
    pallas_call x7, Pallas kernels, call(): pl.pallas_call(kernel, out_shape=out, in_specs=specs, out_specs=jax.tree....  35.8 us
    all_to_all x3, starting transfers between devices, exchange(): return lax.all_to_all(x, 'rows', split_axis=0, concat_axis=0, tiled=True)  26.5 us
    ppermute x1, waiting for transfers between devices, steps(): lax.ppermute(own, 'irrep', [(i, i ^ irreps // 2) for i in range(irreps)])  14.2 us
    unnamed x26, local copies, waits for them, and re-layouts  7.14 us
  transfers between devices with their start and end apart: 4, of which 3 were waited for; matrix products, arithmetic and copies ran while one was open for 2% of the time, Pallas kernels for 18%

profile of v1, /device:TPU:4, one launch (start us, length us, event | category | flops | bytes accessed | tf_op | source)
XLA Modules:
  0.0 122.0 jit_solution(3901861650200147381)
XLA Ops:
  0.0 1.3 %copy-done.1 = f32[1,80,2560]{2,1,0:T(8,128)S(1)} copy-done((f32[1,80,2560]{2,1,0:T(8,128)S(1)}, f32[1,80,2560]{2,1,0:T(8,128)}, u32[]{:S(2)}) %copy-start.1) | copy-done | bytes 819224
  1.3 2.5 %shard_map.39 = f32[32,56,128]{2,1,0:T(8,128)} custom-call(f32[80,2560]{1,0:T(8,128)S(1)} %bitcast.12), custom_call_target="tpu_custom_call" | custom-call | flops 1048576 | bytes 819200 | tf_op jit(solution)/shard_map/pallas_call | solution.py:247
  3.8 11.5 %all-to-all-start.1 = ((f32[32,56,128]{2,1,0:T(8,128)}), f32[32,56,128]{2,1,0:T(8,128)S(1)}, u32[]{:S(2)}, u32[]{:S(2)}) async-start(f32[32,56,128]{2,1,0:T(8,128)} %shard_map.39), calls=%async_computation.1 | async-start | bytes 1835008 | tf_op jit(solution)/shard_map/all_to_all | solution.py:276
  15.3 0.6 collective-permute-start
  15.9 0.0 copy-done.11
  15.9 0.4 convert_reduce_fusion.1
  16.4 0.0 copy-done
  16.4 2.0 %shard_map.37 = (bf16[384,1024]{1,0:T(8,128)(2,1)S(1)}, bf16[384,1024]{1,0:T(8,128)(2,1)S(1)}, bf16[384,1024]{1,0:T(8,128)(2,1)S(1)}, bf16[384,1024]{1,0:T(8,128)(2,1)S(1)}) custom-call(f32[4,8,128,128]{3,2,1,0:T(8,128)S(1)} %bitcast.10), custom_call_target="tpu_custom_call" | custom-call | flops 1048576 | bytes 2097152 | tf_op jit(solution)/shard_map/pallas_call | solution.py:247
  18.5 0.0 copy-start.3
  18.5 0.9 copy-done.3
  19.4 0.9 copy-done.5
  20.3 0.9 copy-done.7
  21.1 0.1 select_reduce_fusion.2.starts_ref
  21.2 0.1 select_reduce_fusion.1
  21.4 0.7 convert_reduce_fusion
  22.1 0.5 select_reduce_fusion.words_ref
  22.6 14.2 %collective-permute-done.c_ref = f32[80,2560]{1,0:T(8,128)S(1)} collective-permute-done((f32[80,2560]{1,0:T(8,128)}, f32[80,2560]{1,0:T(8,128)S(1)}, u32[]{:S(2)}, u32[]{:S(2)}) %collective-permute-start) | collective-permute-done | bytes 819232 | tf_op jit(solution)/shard_map/ppermute | solution.py:278
  36.8 7.9 %shard_map.38 = f32[32,56,128]{2,1,0:T(8,128)} custom-call(s32[4,512]{1,0:T(4,128)S(1)} %select_reduce_fusion.words_ref, s32[4,21]{1,0:T(4,128)S(1)} %select_reduce_fusion.2.starts_ref, f32[80,2560]{1,0:T(8,128)S(1)} %collective-permute-done.c_ref, bf16[384,1024]{1,0:T(8,128)(2,1)S(1)} %get-tuple-element.9.weights_ref), custom_call_target="tpu_custom_call" | custom-call | flops 1258291200 | bytes 1614160 | tf_op jit(solution)/shard_map/pallas_call | solution.py:247
  44.7 0.0 all-to-all-done.1.recv_ref
  44.7 9.5 %all-to-all-start = ((f32[32,56,128]{2,1,0:T(8,128)}), f32[32,56,128]{2,1,0:T(8,128)S(1)}, u32[]{:S(2)}, u32[]{:S(2)}) async-start(f32[32,56,128]{2,1,0:T(8,128)} %shard_map.38), calls=%async_computation | async-start | bytes 1835008 | tf_op jit(solution)/shard_map/all_to_all | solution.py:276
  54.2 0.0 copy-done.8
  54.2 6.3 %shard_map.40.own_ref = f32[20,80,128]{2,1,0:T(8,128)S(1)} custom-call(s32[4,512]{1,0:T(4,128)S(1)} %select_reduce_fusion.words_ref, s32[4,21]{1,0:T(4,128)S(1)} %select_reduce_fusion.2.starts_ref, f32[32,56,128]{2,1,0:T(8,128)S(1)} %all-to-all-done.1.recv_ref, bf16[384,1024]{1,0:T(8,128)(2,1)S(1)} %copy-done.8), custom_call_target="tpu_custom_call" | custom-call | flops 1258291200 | bytes 1712464 | tf_op jit(solution)/shard_map/pallas_call | solution.py:247
  60.5 0.0 copy-start.9
  60.5 0.9 copy-done.9
  61.4 16.8 %all-to-all-done.recv_ref = f32[32,56,128]{2,1,0:T(8,128)S(1)} async-done(((f32[32,56,128]{2,1,0:T(8,128)}), f32[32,56,128]{2,1,0:T(8,128)S(1)}, u32[]{:S(2)}, u32[]{:S(2)}) %all-to-all-start) | async-done | bytes 917536 | tf_op jit(solution)/shard_map/all_to_all | solution.py:276
  78.2 1.1 copy-done.6
  79.4 1.1 copy-done.10
  80.5 9.2 %shard_map.41 = f32[32,56,128]{2,1,0:T(8,128)} custom-call(s32[4,512]{1,0:T(4,128)S(1)} %select_reduce_fusion.words_ref, s32[4,21]{1,0:T(4,128)S(1)} %select_reduce_fusion.2.starts_ref, f32[32,56,128]{2,1,0:T(8,128)S(1)} %all-to-all-done.recv_ref, bf16[384,1024]{1,0:T(8,128)(2,1)S(1)} %copy-done.6, f32[20,80,128]{2,1,0:T(8,128)S(1)} %copy-done.10), custom_call_target="tpu_custom_call" | custom-call | flops 1258291200 | bytes 2531664 | tf_op jit(solution)/shard_map/pallas_call | solution.py:247
  89.7 5.5 %all-to-all-start.2 = ((f32[32,56,128]{2,1,0:T(8,128)}), f32[32,56,128]{2,1,0:T(8,128)S(1)}, u32[]{:S(2)}, u32[]{:S(2)}) async-start(f32[32,56,128]{2,1,0:T(8,128)} %shard_map.41), calls=%async_computation.2 | async-start | bytes 1835008 | tf_op jit(solution)/shard_map/all_to_all | solution.py:276
  95.2 5.4 %shard_map.42.beta_ref = f32[20,80,128]{2,1,0:T(8,128)S(1)} custom-call(s32[4,512]{1,0:T(4,128)S(1)} %select_reduce_fusion.words_ref, s32[4,21]{1,0:T(4,128)S(1)} %select_reduce_fusion.2.starts_ref, f32[80,2560]{1,0:T(8,128)S(1)} %bitcast.13, bf16[384,1024]{1,0:T(8,128)(2,1)S(1)} %copy-done.4), custom_call_target="tpu_custom_call" | custom-call | flops 1258291200 | bytes 1614160 | tf_op jit(solution)/shard_map/pallas_call | solution.py:247
  100.6 19.0 %all-to-all-done.2.recv_ref = f32[32,56,128]{2,1,0:T(8,128)S(1)} async-done(((f32[32,56,128]{2,1,0:T(8,128)}), f32[32,56,128]{2,1,0:T(8,128)S(1)}, u32[]{:S(2)}, u32[]{:S(2)}) %all-to-all-start.2) | async-done | bytes 917536 | tf_op jit(solution)/shard_map/all_to_all | solution.py:276
  119.6 2.4 %shard_map.43 = f32[80,2560]{1,0:T(8,128)} custom-call(f32[32,56,128]{2,1,0:T(8,128)S(1)} %all-to-all-done.2.recv_ref, f32[20,80,128]{2,1,0:T(8,128)S(1)} %shard_map.42.beta_ref), custom_call_target="tpu_custom_call" | custom-call | flops 1048576 | bytes 1736704 | tf_op jit(solution)/shard_map/pallas_call | solution.py:247
  (19 shorter events, 0.1 us)
Async XLA Ops:
  0.0 16.4 %copy-start = (f32[1,4,8,128,128]{4,3,2,1,0:T(8,128)S(1)}, f32[1,4,8,128,128]{4,3,2,1,0:T(8,128)}, u32[]{:S(2)}) copy-start(f32[1,4,8,128,128]{4,3,2,1,0:T(8,128)} %param.5) | copy-start | bytes 6291460
  0.0 1.3 %copy-start.1 = (f32[1,80,2560]{2,1,0:T(8,128)S(1)}, f32[1,80,2560]{2,1,0:T(8,128)}, u32[]{:S(2)}) copy-start(f32[1,80,2560]{2,1,0:T(8,128)} %param.3) | copy-start | bytes 2457604
  1.3 14.6 %copy-start.11 = (s32[1,4,4,320]{3,2,1,0:T(4,128)S(1)}, s32[1,4,4,320]{3,2,1,0:T(4,128)}, u32[]{:S(2)}) copy-start(s32[1,4,4,320]{3,2,1,0:T(4,128)} %param.4) | copy-start | bytes 61444
  3.8 40.9 %all-to-all-start.1 = ((f32[32,56,128]{2,1,0:T(8,128)}), f32[32,56,128]{2,1,0:T(8,128)S(1)}, u32[]{:S(2)}, u32[]{:S(2)}) async-start(f32[32,56,128]{2,1,0:T(8,128)} %shard_map.39), calls=%async_computation.1 | async-start | bytes 1835008 | tf_op jit(solution)/shard_map/all_to_all | solution.py:276
  15.3 21.5 %collective-permute-start = (f32[80,2560]{1,0:T(8,128)}, f32[80,2560]{1,0:T(8,128)S(1)}, u32[]{:S(2)}, u32[]{:S(2)}) collective-permute-start(f32[80,2560]{1,0:T(8,128)} %bitcast.11), channel_id=1, source_target_pairs={{0,4},{1,5},{2,6},{3,7},{4,0},{5,1},{6,2},{7,3},{8,12},{9,13},{10,... | collective-permute-start | bytes 2457608 | tf_op jit(solution)/shard_map/ppermute | solution.py:278
  18.5 0.9 copy-start.3
  19.4 0.9 copy-start.5
  20.3 0.9 copy-start.7
  36.8 17.4 %copy-start.8 = (bf16[384,1024]{1,0:T(8,128)(2,1)S(1)}, bf16[384,1024]{1,0:T(8,128)(2,1)}, u32[]{:S(2)}) copy-start(bf16[384,1024]{1,0:T(8,128)(2,1)} %copy-done.7) | copy-start | bytes 2359300
  44.7 33.5 %all-to-all-start = ((f32[32,56,128]{2,1,0:T(8,128)}), f32[32,56,128]{2,1,0:T(8,128)S(1)}, u32[]{:S(2)}, u32[]{:S(2)}) async-start(f32[32,56,128]{2,1,0:T(8,128)} %shard_map.38), calls=%async_computation | async-start | bytes 1835008 | tf_op jit(solution)/shard_map/all_to_all | solution.py:276
  60.5 0.9 copy-start.9
  78.2 1.1 copy-start.6
  79.4 1.1 copy-start.10
  80.5 14.7 %copy-start.2 = (f32[1,80,2560]{2,1,0:T(8,128)S(1)}, f32[1,80,2560]{2,1,0:T(8,128)}, u32[]{:S(2)}) copy-start(f32[1,80,2560]{2,1,0:T(8,128)} %param.3) | copy-start | bytes 2457604
  80.5 14.7 %copy-start.4 = (bf16[384,1024]{1,0:T(8,128)(2,1)S(1)}, bf16[384,1024]{1,0:T(8,128)(2,1)}, u32[]{:S(2)}) copy-start(bf16[384,1024]{1,0:T(8,128)(2,1)} %copy-done.3) | copy-start | bytes 2359300
  89.7 29.9 %all-to-all-start.2 = ((f32[32,56,128]{2,1,0:T(8,128)}), f32[32,56,128]{2,1,0:T(8,128)S(1)}, u32[]{:S(2)}, u32[]{:S(2)}) async-start(f32[32,56,128]{2,1,0:T(8,128)} %shard_map.41), calls=%async_computation.2 | async-start | bytes 1835008 | tf_op jit(solution)/shard_map/all_to_all | solution.py:276

commit v2 on v1

--- a/solution.py
+++ b/solution.py
@@ -7,7 +7,7 @@
 
 
 LANES = 128
-PACKED = 56
+PACKED = 50
 GROUP = 8
 RUN = 8
 f32, bf16 = jnp.float32, jnp.bfloat16
@@ -23,26 +23,48 @@
     return value if shift == 0 else pltpu.roll(value, shift, 1)
 
 
-def pack(z):
+CORNER = 16
+
+
+def sublane():
+    return lax.broadcasted_iota(jnp.int32, (8, LANES), 0)
+
+
+def put(send_ref, d, z):
     by32, by64, by80 = rolled(z[48:64], 32), rolled(z[64:80], 64), rolled(z[48:80], 80)
-    top = jnp.where(lane_of(32) < 80, z[0:32], by80)
-    middle = jnp.where(lane_of(16) < 80, z[32:48], jnp.where(lane_of(16) < 112, by32, by64))
-    bottom = jnp.where(lane_of(8) < 16, by64[0:8], by80[24:32])
-    return jnp.concatenate([top, middle, bottom], axis=0)
-
-
-def unpack(p):
+    send_ref[pl.ds(d * PACKED, 32), :] = jnp.where(lane_of(32) < 80, z[0:32], by80)
+    send_ref[pl.ds(d * PACKED + 32, 16), :] = jnp.where(
+        lane_of(16) < 80, z[32:48], jnp.where(lane_of(16) < 112, by32, by64)
+    )
+    for a in range(2):
+        slanted = pltpu.roll(by64[8 * a : 8 * a + 8], 0, 1, stride=CORNER, stride_axis=0)
+        send_ref[pl.ds(d * PACKED + 48 + a, 1), :] = jnp.sum(
+            jnp.where(lane_of(8) // CORNER == sublane(), slanted, 0.0), axis=0, keepdims=True
+        )
+
+
+def get(recv_ref, s):
+    p = recv_ref[pl.ds(s * PACKED, 48), :]
     by48 = rolled(p[0:32], 48)
     rows48 = jnp.where(lane_of(16) < 48, by48[0:16], rolled(p[32:48], 96))
     tail = rolled(p[32:48], 64)
     lane = lane_of(8)
-    rows64 = jnp.where(lane < 48, by48[16:24], jnp.where(lane < 64, tail[0:8], rolled(p[48:56], 64)))
-    rows72 = jnp.where(lane < 48, by48[24:32], jnp.where(lane < 64, tail[8:16], rolled(p[48:56], 48)))
-    return jnp.concatenate([p[0:48], rows48, rows64, rows72], axis=0)
+    last = []
+    for a in range(2):
+        line = jnp.broadcast_to(recv_ref[pl.ds(s * PACKED + 48 + a, 1), :], (8, LANES))
+        corner = rolled(line, 64)
+        for bit in (1, 2, 4):
+            corner = jnp.where(sublane() & bit > 0, rolled(corner, -bit * CORNER), corner)
+        at = slice(8 * a, 8 * a + 8)
+        last.append(
+            jnp.where(lane < 48, by48[16 + 8 * a : 24 + 8 * a], jnp.where(lane < 64, tail[at], corner))
+        )
+    return jnp.concatenate([p[0:48], rows48, *last], axis=0)
 
 
 def send_transposed(tile_at, count, send_ref, turned_ref):
-    rows = turned_ref.shape[0] // send_ref.shape[0]
+    shards = send_ref.shape[0] // PACKED
+    rows = turned_ref.shape[0] // shards
 
     def turn(j, _):
         turned_ref[pl.ds(pl.multiple_of(j * LANES, LANES), LANES), 0:rows] = tile_at(j).T
@@ -51,10 +73,10 @@
     lax.fori_loop(0, count, turn, 0, unroll=5)
 
     def one(d, _):
-        send_ref[d] = pack(turned_ref[pl.ds(pl.multiple_of(d * rows, 8), rows), :])
-        return 0
-
-    lax.fori_loop(0, send_ref.shape[0], one, 0, unroll=4)
+        put(send_ref, d, turned_ref[pl.ds(pl.multiple_of(d * rows, 8), rows), :])
+        return 0
+
+    lax.fori_loop(0, shards, one, 0, unroll=4)
 
 
 def split_into(lhs_ref, j, value):
@@ -72,7 +94,7 @@
 
     def group(g, _):
         for c in range(GROUP):
-            pieces_ref[c] = unpack(recv_ref[g * GROUP + c])
+            pieces_ref[c] = get(recv_ref, g * GROUP + c)
         for b in range(GROUP * rows // LANES):
             first, last = b * LANES // rows, (b * LANES + LANES - 1) // rows
             value = rolled(pieces_ref[last], last * rows - b * LANES)
@@ -84,7 +106,7 @@
             split_into(lhs_ref, g * (GROUP * rows // LANES) + b, value)
         return 0
 
-    lax.fori_loop(0, recv_ref.shape[0] // GROUP, group, 0)
+    lax.fori_loop(0, recv_ref.shape[0] // PACKED // GROUP, group, 0)
 
 
 def send_rows(sum_ref, send_ref):
@@ -99,10 +121,10 @@
                 value = jnp.where(
                     lane_of(rows) < LANES - o, value, rolled(sum_ref[base + b + 1], -o)
                 )
-            send_ref[g * GROUP + c] = pack(value)
-        return 0
-
-    lax.fori_loop(0, send_ref.shape[0] // GROUP, group, 0)
+            put(send_ref, g * GROUP + c, value)
+        return 0
+
+    lax.fori_loop(0, send_ref.shape[0] // PACKED // GROUP, group, 0)
 
 
 def operate(which_op, words_ref, starts_ref, weights_ref, lhs_ref, products_ref, sum_ref, first):
@@ -198,26 +220,58 @@
     return lambda i: jnp.zeros(ref.shape[1:], f32)
 
 
-def beta_kernel(words_ref, starts_ref, c_ref, weights_ref, sum_ref, lhs_ref, products_ref):
+def beta_kernel(words_ref, starts_ref, c_ref, w_ref, sum_ref, lhs_ref, products_ref, weights_ref, sem):
+    fetch = pltpu.make_async_copy(w_ref, weights_ref, sem)
+    fetch.start()
     split_all(c_ref, lhs_ref)
+    fetch.wait()
     operate(0, words_ref, starts_ref, weights_ref, lhs_ref, products_ref, sum_ref, zeros_like_block(sum_ref))
 
 
-def mixed_kernel(words_ref, starts_ref, c_ref, weights_ref, send_ref, lhs_ref, products_ref, sum_ref, turned_ref):
+def mixed_kernel(
+    words_ref, starts_ref, c_ref, w_ref, send_ref, lhs_ref, products_ref, weights_ref, sem, sum_ref, turned_ref
+):
+    fetch = pltpu.make_async_copy(w_ref, weights_ref, sem)
+    fetch.start()
     split_all(c_ref, lhs_ref)
+    fetch.wait()
     operate(3, words_ref, starts_ref, weights_ref, lhs_ref, products_ref, sum_ref, zeros_like_block(sum_ref))
     send_transposed(lambda j: sum_ref[j], sum_ref.shape[0], send_ref, turned_ref)
 
 
-def alpha_kernel(words_ref, starts_ref, recv_ref, weights_ref, sum_ref, lhs_ref, products_ref, pieces_ref):
+def alpha_kernel(
+    words_ref, starts_ref, recv_ref, w_ref, sum_ref, lhs_ref, products_ref, weights_ref, sem, pieces_ref
+):
+    fetch = pltpu.make_async_copy(w_ref, weights_ref, sem)
+    fetch.start()
     receive_rows(recv_ref, pieces_ref, lhs_ref)
+    fetch.wait()
     operate(1, words_ref, starts_ref, weights_ref, lhs_ref, products_ref, sum_ref, zeros_like_block(sum_ref))
 
 
 def cross_kernel(
-    words_ref, starts_ref, recv_ref, weights_ref, own_ref, send_ref, lhs_ref, products_ref, pieces_ref, sum_ref
+    words_ref,
+    starts_ref,
+    recv_ref,
+    w_ref,
+    alpha_ref,
+    send_ref,
+    lhs_ref,
+    products_ref,
+    weights_ref,
+    sem,
+    pieces_ref,
+    sum_ref,
+    own_ref,
+    own_sem,
 ):
+    fetch = pltpu.make_async_copy(w_ref, weights_ref, sem)
+    fetch.start()
+    fetch_own = pltpu.make_async_copy(alpha_ref, own_ref, own_sem)
+    fetch_own.start()
     receive_rows(recv_ref, pieces_ref, lhs_ref)
+    fetch.wait()
+    fetch_own.wait()
     operate(2, words_ref, starts_ref, weights_ref, lhs_ref, products_ref, sum_ref, lambda i: own_ref[i])
     send_rows(sum_ref, send_ref)
 
@@ -226,10 +280,10 @@
     rows = out_ref.shape[0]
 
     def one(d, _):
-        turned_ref[pl.ds(pl.multiple_of(d * rows, 8), rows), :] = unpack(recv_ref[d])
-        return 0
-
-    lax.fori_loop(0, recv_ref.shape[0], one, 0, unroll=4)
+        turned_ref[pl.ds(pl.multiple_of(d * rows, 8), rows), :] = get(recv_ref, d)
+        return 0
+
+    lax.fori_loop(0, recv_ref.shape[0] // PACKED, one, 0, unroll=4)
 
     def turn(j, _):
         back = turned_ref[pl.ds(pl.multiple_of(j * LANES, LANES), LANES), :].T
@@ -239,9 +293,12 @@
     lax.fori_loop(0, beta_ref.shape[0], turn, 0, unroll=5)
 
 
-def call(kernel, out, scratch, operands, flops):
+def call(kernel, out, scratch, operands, flops, fetched=()):
     specs = [
-        pl.BlockSpec(memory_space=SMEM if x.dtype == jnp.int32 else VMEM) for x in operands
+        pl.BlockSpec(
+            memory_space=SMEM if x.dtype == jnp.int32 else pl.ANY if at in fetched else VMEM
+        )
+        for at, x in enumerate(operands)
     ]
     moved = sum(x.size * x.dtype.itemsize for x in operands)
     return pl.pallas_call(
@@ -250,7 +307,7 @@
         in_specs=specs,
         out_specs=jax.tree.map(lambda _: pl.BlockSpec(memory_space=VMEM), out),
         scratch_shapes=scratch,
-        compiler_params=pltpu.CompilerParams(vmem_limit_bytes=20 << 20),
+        compiler_params=pltpu.CompilerParams(vmem_limit_bytes=52 << 20),
         cost_estimate=pl.CostEstimate(flops=flops, bytes_accessed=moved, transcendentals=0),
     )(*operands)
 
@@ -263,27 +320,37 @@
     blocks, tile_count = width // LANES, tiles.shape[1]
     flops = 6 * rows * blocks * LANES * LANES * tile_count
 
-    packed = jax.ShapeDtypeStruct((shards, PACKED, LANES), f32)
+    packed = jax.ShapeDtypeStruct((shards * PACKED, LANES), f32)
     summed = jax.ShapeDtypeStruct((blocks, rows, LANES), f32)
     lhs = VMEM((blocks * rows, 3 * LANES), bf16)
     products = VMEM((blocks * tile_count, rows, LANES), f32)
     turned = VMEM((width, LANES), f32)
     pieces = VMEM((GROUP, rows, LANES), f32)
     total = VMEM((blocks, rows, LANES), f32)
+    work = [lhs, products, VMEM((3 * LANES, tile_count * LANES), bf16), pltpu.SemaphoreType.DMA]
     weights = jax.ShapeDtypeStruct((3 * LANES, tile_count * LANES), bf16)
 
     def exchange(x):
-        return lax.all_to_all(x, "rows", split_axis=0, concat_axis=0, tiled=True)
+        x = x.reshape(shards, PACKED // 2, 2, LANES)
+        x = lax.all_to_all(x, "rows", split_axis=0, concat_axis=0, tiled=True)
+        return x.reshape(shards * PACKED, LANES)
 
     partner = lax.ppermute(own, "irrep", [(i, i ^ irreps // 2) for i in range(irreps)])
     listed = runs_of(codes, blocks, tile_count)
     columns_in = exchange(call(format_kernel, packed, [turned], (own,), 1 << 20))
     w0, w1, w2, w3 = call(weights_kernel, [weights] * tiles.shape[0], [], (tiles,), 1 << 20)
-    mixed = call(mixed_kernel, packed, [lhs, products, total, turned], (*listed, partner, w3), flops)
+    mixed = call(mixed_kernel, packed, [*work, total, turned], (*listed, partner, w3), flops, (3,))
     cross_in = exchange(mixed)
-    beta = call(beta_kernel, summed, [lhs, products], (*listed, own, w0), flops)
-    alpha = call(alpha_kernel, summed, [lhs, products, pieces], (*listed, columns_in, w1), flops)
-    cross = call(cross_kernel, packed, [lhs, products, pieces, total], (*listed, cross_in, w2, alpha), flops)
+    beta = call(beta_kernel, summed, work, (*listed, own, w0), flops, (3,))
+    alpha = call(alpha_kernel, summed, [*work, pieces], (*listed, columns_in, w1), flops, (3,))
+    cross = call(
+        cross_kernel,
+        packed,
+        [*work, pieces, total, total, pltpu.SemaphoreType.DMA],
+        (*listed, cross_in, w2, alpha),
+        flops,
+        (3, 4),
+    )
     returned = exchange(cross)
     out = call(final_kernel, jax.ShapeDtypeStruct((rows, width), f32), [turned], (returned, beta), 1 << 20)
     return out[None]

time: 123 us -> 111 us (0.902)
  the two profiles are of different devices: /device:TPU:4 before, /device:TPU:8 now
where the time goes in v2:
time: 111 us
  Pallas kernels  44.1 us (40%)
  waiting for transfers between devices  35.3 us (32%)
  starting transfers between devices  25.9 us (23%)
  local copies, waits for them, and re-layouts  3.23 us (3%)
  other arithmetic  1.94 us (2%)
    pallas_call x7, Pallas kernels, call(): pl.pallas_call(kernel, out_shape=out, in_specs=specs, out_specs=jax.tree....  44.1 us
    all_to_all x3, waiting for transfers between devices, exchange(): x = lax.all_to_all(x, 'rows', split_axis=0, concat_axis=0, tiled=True)  35.3 us
    all_to_all x3, starting transfers between devices, exchange(): x = lax.all_to_all(x, 'rows', split_axis=0, concat_axis=0, tiled=True)  22.9 us
    unnamed x14, local copies, waits for them, and re-layouts  3.23 us
    ppermute x1, starting transfers between devices, steps(): lax.ppermute(own, 'irrep', [(i, i ^ irreps // 2) for i in range(irreps)])  3.02 us
  transfers between devices with their start and end apart: 4, of which 3 were waited for; matrix products, arithmetic and copies ran while one was open for 2% of the time, Pallas kernels for 27%

profile of v2, /device:TPU:8, one launch (start us, length us, event | category | flops | bytes accessed | tf_op | source)
XLA Modules:
  0.0 110.7 jit_solution(17858805205718474853)
XLA Ops:
  0.0 3.0 %collective-permute-start = (f32[80,2560]{1,0:T(8,128)}, f32[80,2560]{1,0:T(8,128)}, u32[]{:S(2)}, u32[]{:S(2)}) collective-permute-start(f32[80,2560]{1,0:T(8,128)} %bitcast.17), channel_id=1, source_target_pairs={{0,4},{1,5},{2,6},{3,7},{4,0},{5,1},{6,2},{7,3},{8,12},{9,13},{10,... | collective-permute-start | bytes 2457608 | tf_op jit(solution)/shard_map/ppermute | solution.py:338
  3.0 0.0 copy-start
  3.0 1.2 %copy-done = f32[1,80,2560]{2,1,0:T(8,128)S(1)} copy-done((f32[1,80,2560]{2,1,0:T(8,128)S(1)}, f32[1,80,2560]{2,1,0:T(8,128)}, u32[]{:S(2)}) %copy-start) | copy-done | bytes 819224
  4.2 0.0 copy-start.5
  4.2 2.8 %shard_map.39 = f32[1600,128]{1,0:T(8,128)} custom-call(f32[80,2560]{1,0:T(8,128)S(1)} %bitcast.19), custom_call_target="tpu_custom_call" | custom-call | flops 1048576 | bytes 819200 | tf_op jit(solution)/shard_map/pallas_call | solution.py:304
  7.0 11.7 %all-to-all-start.1 = ((f32[32,25,2,128]{3,2,1,0:T(2,128)}), f32[32,25,2,128]{3,2,1,0:T(2,128)S(1)}, u32[]{:S(2)}, u32[]{:S(2)}) async-start(f32[32,25,2,128]{3,2,1,0:T(2,128)} %bitcast.5), calls=%async_computation.1 | async-start | bytes 1638400 | tf_op jit(solution)/shard_map/all_to_all | solution.py:335
  18.7 0.0 copy-done.5
  18.8 0.4 convert_reduce_fusion.1
  19.3 4.7 %shard_map.37 = (bf16[384,1024]{1,0:T(8,128)(2,1)S(1)}, bf16[384,1024]{1,0:T(8,128)(2,1)S(1)}, bf16[384,1024]{1,0:T(8,128)(2,1)}, bf16[384,1024]{1,0:T(8,128)(2,1)}) custom-call(f32[4,8,128,128]{3,2,1,0:T(8,128)} %bitcast.20), custom_call_target="tpu_custom_call" | custom-call | flops 1048576 | bytes 2097152 | tf_op jit(solution)/shard_map/pallas_call | solution.py:304
  24.0 0.1 select_reduce_fusion.2.starts_ref
  24.1 0.1 select_reduce_fusion.1
  24.2 0.7 convert_reduce_fusion
  24.9 0.5 select_reduce_fusion.words_ref
  25.4 0.0 collective-permute-done.c_ref
  25.4 0.0 copy-start.2
  25.5 1.1 %copy-done.2 = bf16[384,1024]{1,0:T(8,128)(2,1)S(1)} copy-done((bf16[384,1024]{1,0:T(8,128)(2,1)S(1)}, bf16[384,1024]{1,0:T(8,128)(2,1)}, u32[]{:S(2)}) %copy-start.2) | copy-done | bytes 786456
  26.6 8.9 %shard_map.38 = f32[1600,128]{1,0:T(8,128)} custom-call(s32[4,512]{1,0:T(4,128)S(1)} %select_reduce_fusion.words_ref, s32[4,21]{1,0:T(4,128)S(1)} %select_reduce_fusion.2.starts_ref, f32[80,2560]{1,0:T(8,128)} %collective-permute-done.c_ref, bf16[384,1024]{1,0:T(8,128)(2,1)S(1)} %copy-done.2), custom_call_target="tpu_custom_call" | custom-call | flops 1258291200 | bytes 1614160 | tf_op jit(solution)/shard_map/pallas_call | solution.py:304
  35.5 6.1 %all-to-all-done.1 = f32[32,25,2,128]{3,2,1,0:T(2,128)S(1)} async-done(((f32[32,25,2,128]{3,2,1,0:T(2,128)}), f32[32,25,2,128]{3,2,1,0:T(2,128)S(1)}, u32[]{:S(2)}, u32[]{:S(2)}) %all-to-all-start.1) | async-done | bytes 819232 | tf_op jit(solution)/shard_map/all_to_all | solution.py:335
  41.6 0.0 copy-start.4
  41.6 5.6 %all-to-all-start = ((f32[32,25,2,128]{3,2,1,0:T(2,128)}), f32[32,25,2,128]{3,2,1,0:T(2,128)}, u32[]{:S(2)}, u32[]{:S(2)}) async-start(f32[32,25,2,128]{3,2,1,0:T(2,128)} %bitcast.3), calls=%async_computation | async-start | bytes 1638400 | tf_op jit(solution)/shard_map/all_to_all | solution.py:335
  47.2 0.0 copy-done.4
  47.3 0.0 copy-start.1
  47.3 7.6 %shard_map.40.alpha_ref = f32[20,80,128]{2,1,0:T(8,128)S(1)} custom-call(s32[4,512]{1,0:T(4,128)S(1)} %select_reduce_fusion.words_ref, s32[4,21]{1,0:T(4,128)S(1)} %select_reduce_fusion.2.starts_ref, f32[1600,128]{1,0:T(8,128)} %bitcast.21, bf16[384,1024]{1,0:T(8,128)(2,1)S(1)} %get-tuple-element.11.w_ref), custom_call_target="tpu_custom_call" | custom-call | flops 1258291200 | bytes 1614160 | tf_op jit(solution)/shard_map/pallas_call | solution.py:304
  54.8 0.0 copy-start.3
  54.9 0.9 copy-done.3
  55.8 13.5 %all-to-all-done = f32[32,25,2,128]{3,2,1,0:T(2,128)} async-done(((f32[32,25,2,128]{3,2,1,0:T(2,128)}), f32[32,25,2,128]{3,2,1,0:T(2,128)}, u32[]{:S(2)}, u32[]{:S(2)}) %all-to-all-start) | async-done | bytes 819232 | tf_op jit(solution)/shard_map/all_to_all | solution.py:335
  69.3 0.0 copy-done.1
  69.3 10.4 %shard_map.41 = f32[1600,128]{1,0:T(8,128)} custom-call(s32[4,512]{1,0:T(4,128)S(1)} %select_reduce_fusion.words_ref, s32[4,21]{1,0:T(4,128)S(1)} %select_reduce_fusion.2.starts_ref, f32[1600,128]{1,0:T(8,128)} %bitcast.4.recv_ref, bf16[384,1024]{1,0:T(8,128)(2,1)S(1)} %copy-done.1, f32[20,80,128]{2,1,0:T(8,128)} %copy-done.3), custom_call_target="tpu_custom_call" | custom-call | flops 1258291200 | bytes 2433360 | tf_op jit(solution)/shard_map/pallas_call | solution.py:304
  79.7 5.6 %all-to-all-start.2 = ((f32[32,25,2,128]{3,2,1,0:T(2,128)}), f32[32,25,2,128]{3,2,1,0:T(2,128)S(1)}, u32[]{:S(2)}, u32[]{:S(2)}) async-start(f32[32,25,2,128]{3,2,1,0:T(2,128)} %bitcast.7), calls=%async_computation.2 | async-start | bytes 1638400 | tf_op jit(solution)/shard_map/all_to_all | solution.py:335
  85.2 5.9 %shard_map.42.beta_ref = f32[20,80,128]{2,1,0:T(8,128)S(1)} custom-call(s32[4,512]{1,0:T(4,128)S(1)} %select_reduce_fusion.words_ref, s32[4,21]{1,0:T(4,128)S(1)} %select_reduce_fusion.2.starts_ref, f32[80,2560]{1,0:T(8,128)} %bitcast.18, bf16[384,1024]{1,0:T(8,128)(2,1)S(1)} %get-tuple-element.12.w_ref), custom_call_target="tpu_custom_call" | custom-call | flops 1258291200 | bytes 1614160 | tf_op jit(solution)/shard_map/pallas_call | solution.py:304
  91.2 15.7 %all-to-all-done.2 = f32[32,25,2,128]{3,2,1,0:T(2,128)S(1)} async-done(((f32[32,25,2,128]{3,2,1,0:T(2,128)}), f32[32,25,2,128]{3,2,1,0:T(2,128)S(1)}, u32[]{:S(2)}, u32[]{:S(2)}) %all-to-all-start.2) | async-done | bytes 819232 | tf_op jit(solution)/shard_map/all_to_all | solution.py:335
  106.9 3.8 %shard_map.43 = f32[80,2560]{1,0:T(8,128)} custom-call(f32[1600,128]{1,0:T(8,128)S(1)} %bitcast.16, f32[20,80,128]{2,1,0:T(8,128)S(1)} %shard_map.42.beta_ref), custom_call_target="tpu_custom_call" | custom-call | flops 1048576 | bytes 1638400 | tf_op jit(solution)/shard_map/pallas_call | solution.py:304
  (7 shorter events, 0.1 us)
Async XLA Ops:
  0.0 25.4 %collective-permute-start = (f32[80,2560]{1,0:T(8,128)}, f32[80,2560]{1,0:T(8,128)}, u32[]{:S(2)}, u32[]{:S(2)}) collective-permute-start(f32[80,2560]{1,0:T(8,128)} %bitcast.17), channel_id=1, source_target_pairs={{0,4},{1,5},{2,6},{3,7},{4,0},{5,1},{6,2},{7,3},{8,12},{9,13},{10,... | collective-permute-start | bytes 2457608 | tf_op jit(solution)/shard_map/ppermute | solution.py:338
  3.0 1.2 %copy-start = (f32[1,80,2560]{2,1,0:T(8,128)S(1)}, f32[1,80,2560]{2,1,0:T(8,128)}, u32[]{:S(2)}) copy-start(f32[1,80,2560]{2,1,0:T(8,128)} %param.3) | copy-start | bytes 2457604
  4.2 14.5 %copy-start.5 = (s32[1,4,4,320]{3,2,1,0:T(4,128)S(1)}, s32[1,4,4,320]{3,2,1,0:T(4,128)}, u32[]{:S(2)}) copy-start(s32[1,4,4,320]{3,2,1,0:T(4,128)} %param.4) | copy-start | bytes 61444
  7.0 34.6 %all-to-all-start.1 = ((f32[32,25,2,128]{3,2,1,0:T(2,128)}), f32[32,25,2,128]{3,2,1,0:T(2,128)S(1)}, u32[]{:S(2)}, u32[]{:S(2)}) async-start(f32[32,25,2,128]{3,2,1,0:T(2,128)} %bitcast.5), calls=%async_computation.1 | async-start | bytes 1638400 | tf_op jit(solution)/shard_map/all_to_all | solution.py:335
  25.4 1.1 %copy-start.2 = (bf16[384,1024]{1,0:T(8,128)(2,1)S(1)}, bf16[384,1024]{1,0:T(8,128)(2,1)}, u32[]{:S(2)}) copy-start(bf16[384,1024]{1,0:T(8,128)(2,1)} %get-tuple-element.9.w_ref) | copy-start | bytes 2359300
  41.6 5.6 %copy-start.4 = (f32[32,25,2,128]{3,2,1,0:T(2,128)}, f32[32,25,2,128]{3,2,1,0:T(2,128)S(1)}, u32[]{:S(2)}) copy-start(f32[32,25,2,128]{3,2,1,0:T(2,128)S(1)} %all-to-all-done.1) | copy-start | bytes 2457604
  41.6 27.7 %all-to-all-start = ((f32[32,25,2,128]{3,2,1,0:T(2,128)}), f32[32,25,2,128]{3,2,1,0:T(2,128)}, u32[]{:S(2)}, u32[]{:S(2)}) async-start(f32[32,25,2,128]{3,2,1,0:T(2,128)} %bitcast.3), calls=%async_computation | async-start | bytes 1638400 | tf_op jit(solution)/shard_map/all_to_all | solution.py:335
  47.3 22.0 %copy-start.1 = (bf16[384,1024]{1,0:T(8,128)(2,1)S(1)}, bf16[384,1024]{1,0:T(8,128)(2,1)}, u32[]{:S(2)}) copy-start(bf16[384,1024]{1,0:T(8,128)(2,1)} %get-tuple-element.10.w_ref) | copy-start | bytes 2359300
  54.8 0.9 copy-start.3
  79.7 27.2 %all-to-all-start.2 = ((f32[32,25,2,128]{3,2,1,0:T(2,128)}), f32[32,25,2,128]{3,2,1,0:T(2,128)S(1)}, u32[]{:S(2)}, u32[]{:S(2)}) async-start(f32[32,25,2,128]{3,2,1,0:T(2,128)} %bitcast.7), calls=%async_computation.2 | async-start | bytes 1638400 | tf_op jit(solution)/shard_map/all_to_all | solution.py:335

commit v3 on v2

v3 whole, which is shorter than its diff:
```python
import jax
import jax.numpy as jnp
from jax import lax
from jax.experimental import pallas as pl
from jax.experimental.pallas import tpu as pltpu
from jax.sharding import PartitionSpec as P


LANES = 128
PACKED = 50
GROUP = 8
RUN = 8
TOGETHER = 2
f32, bf16 = jnp.float32, jnp.bfloat16
VMEM, SMEM = pltpu.VMEM, pltpu.SMEM


def lane_of(rows):
    return lax.broadcasted_iota(jnp.int32, (rows, LANES), 1)


def rolled(value, shift):
    shift %= LANES
    return value if shift == 0 else pltpu.roll(value, shift, 1)


CORNER = 16


def sublane():
    return lax.broadcasted_iota(jnp.int32, (8, LANES), 0)


def put(send_ref, d, z):
    by32, by64, by80 = rolled(z[48:64], 32), rolled(z[64:80], 64), rolled(z[48:80], 80)
    send_ref[pl.ds(d * PACKED, 32), :] = jnp.where(lane_of(32) < 80, z[0:32], by80)
    send_ref[pl.ds(d * PACKED + 32, 16), :] = jnp.where(
        lane_of(16) < 80, z[32:48], jnp.where(lane_of(16) < 112, by32, by64)
    )
    lane = lane_of(8)
    corner = jnp.where(lane < 16, by64[0:8], by80[24:32])
    corner = jnp.where(lane < 32, corner, rolled(pltpu.roll(corner, 4, 0), 32))
    corner = jnp.where(lane < 64, corner, rolled(pltpu.roll(corner, 6, 0), 64))
    send_ref[pl.ds(d * PACKED + 48, 2), :] = corner[0:2]


def get(recv_ref, s):
    p = recv_ref[pl.ds(s * PACKED, 48), :]
    by48 = rolled(p[0:32], 48)
    rows48 = jnp.where(lane_of(16) < 48, by48[0:16], rolled(p[32:48], 96))
    tail = rolled(p[32:48], 64)
    two = recv_ref[pl.ds(s * PACKED + 48, 2), :]
    corner = jnp.concatenate([two, two, two, two], axis=0)
    lane = lane_of(8)
    corner = jnp.where(sublane() & 2 > 0, rolled(corner, 64), corner)
    corner = jnp.where(sublane() & 4 > 0, rolled(corner, 96), corner)
    last = []
    for a in range(2):
        at = slice(8 * a, 8 * a + 8)
        last.append(
            jnp.where(
                lane < 48,
                by48[16 + 8 * a : 24 + 8 * a],
                jnp.where(lane < 64, tail[at], rolled(corner, 64 - CORNER * a)),
            )
        )
    return jnp.concatenate([p[0:48], rows48, *last], axis=0)


def send_transposed(tile_at, count, send_ref, turned_ref):
    rows = turned_ref.shape[0] * PACKED // send_ref.shape[0]

    def turn(j, _):
        turned_ref[pl.ds(pl.multiple_of(j * LANES, LANES), LANES), 0:rows] = tile_at(j).T
        return 0

    lax.fori_loop(0, count, turn, 0, unroll=5)
    send_turned(send_ref, turned_ref)


def send_turned(send_ref, turned_ref):
    shards = send_ref.shape[0] // PACKED
    rows = turned_ref.shape[0] // shards

    def one(d, _):
        put(send_ref, d, turned_ref[pl.ds(pl.multiple_of(d * rows, 8), rows), :])
        return 0

    lax.fori_loop(0, shards, one, 0, unroll=8)


def split_into(lhs_ref, j, value):
    rows = value.shape[0]
    high = value.astype(bf16)
    low = (value - high.astype(f32)).astype(bf16)
    at = pl.ds(pl.multiple_of(j * rows, 16), rows)
    lhs_ref[at, 0:128] = high
    lhs_ref[at, 128:256] = low
    lhs_ref[at, 256:384] = high


def receive_rows(recv_ref, pieces_ref, lhs_ref):
    rows = pieces_ref.shape[1]

    def group(g, _):
        for c in range(GROUP):
            pieces_ref[c] = get(recv_ref, g * GROUP + c)
        for b in range(GROUP * rows // LANES):
            first, last = b * LANES // rows, (b * LANES + LANES - 1) // rows
            value = rolled(pieces_ref[last], last * rows - b * LANES)
            for c in range(last - 1, first - 1, -1):
                end = c * rows + rows - b * LANES
                value = jnp.where(
                    lane_of(rows) < end, rolled(pieces_ref[c], c * rows - b * LANES), value
                )
            split_into(lhs_ref, g * (GROUP * rows // LANES) + b, value)
        return 0

    lax.fori_loop(0, recv_ref.shape[0] // PACKED // GROUP, group, 0)


def send_rows(sum_ref, send_ref):
    rows = sum_ref.shape[1]

    def group(g, _):
        base = g * (GROUP * rows // LANES)
        for c in range(GROUP):
            b, o = c * rows // LANES, c * rows % LANES
            value = rolled(sum_ref[base + b], -o)
            if o + rows > LANES:
                value = jnp.where(
                    lane_of(rows) < LANES - o, value, rolled(sum_ref[base + b + 1], -o)
                )
            put(send_ref, g * GROUP + c, value)
        return 0

    lax.fori_loop(0, send_ref.shape[0] // PACKED // GROUP, group, 0)


def operate(lists, weights_ref, lhs_ref, products_ref, sum_ref, first):
    blocks, rows, _ = sum_ref.shape
    tile_count = products_ref.shape[0] // blocks
    numbers_ref, signs_ref = lists.wait()

    def multiply(n, _):
        at = pl.ds(pl.multiple_of(n * 2 * LANES, 2 * LANES), 2 * LANES)
        both = jnp.dot(lhs_ref[...], weights_ref[:, at], preferred_element_type=f32)
        for j in range(blocks):
            for half in range(2):
                products_ref[j * tile_count + 2 * n + half] = both[
                    j * rows : (j + 1) * rows, half * LANES : (half + 1) * LANES
                ]
        return 0

    lax.fori_loop(0, tile_count // 2, multiply, 0)
    for i in range(blocks):
        sum_ref[i] = first(i)
    slots = signs_ref.shape[0]

    def run(q, _):
        added = []
        for r in range(TOGETHER):
            at = (q * TOGETHER + r) * RUN
            total = signs_ref[at] * products_ref[numbers_ref[at]]
            for u in range(1, RUN):
                total = total + signs_ref[at + u] * products_ref[numbers_ref[at + u]]
            added.append(total)
        for r in range(TOGETHER):
            sum_ref[numbers_ref[slots + q * TOGETHER + r]] += added[r]
        return 0

    runs = numbers_ref[slots + slots // RUN]
    lax.fori_loop(0, (runs + TOGETHER - 1) // TOGETHER, run, 0)


def runs_of(block_codes, blocks, tile_count):
    row, column, tile, sign = (block_codes[:, field] for field in range(4))
    words = ((column * tile_count + tile) * blocks + row) * 4 + jnp.where(sign > 0, 1, 2)
    listed = row.shape[1]
    slots = (listed + blocks * (RUN - 1) + (TOGETHER - 1) * RUN + 127) // 128 * 128
    at = jnp.arange(listed, dtype=jnp.int32)
    block = jnp.arange(blocks, dtype=jnp.int32)
    within = jnp.sum(
        (row[:, None, :] == row[:, :, None]) & (at[None, None, :] < at[None, :, None]),
        axis=2,
        dtype=jnp.int32,
    )
    counts = jnp.sum(row[:, None, :] == block[None, :, None], axis=2, dtype=jnp.int32)
    runs = (counts + RUN - 1) // RUN
    begin = jnp.sum(jnp.where(block[None, None, :] < row[:, :, None], runs[:, None, :], 0), axis=2)
    place = begin * RUN + within
    slot = jnp.arange(slots, dtype=jnp.int32)
    grouped = jnp.sum(
        jnp.where(place[:, None, :] == slot[None, :, None], words[:, None, :], 0), axis=2
    )
    signs = ((grouped & 1) - ((grouped >> 1) & 1)).astype(f32)
    pair = grouped >> 2
    targets = (pair % blocks).reshape(pair.shape[0], slots // RUN, RUN)[:, :, 0]
    all_runs = jnp.sum(runs, axis=1, keepdims=True)
    numbers = jnp.concatenate([pair // blocks, targets, all_runs], axis=1)
    numbers = jnp.pad(numbers, ((0, 0), (0, -numbers.shape[1] % LANES)))
    return numbers.astype(jnp.int32), signs


class Lists:
    def __init__(self, which_op, given, held, sems):
        self.held = held
        self.copies = [
            pltpu.make_async_copy(source.at[which_op], target, sems.at[at])
            for at, (source, target) in enumerate(zip(given, held))
        ]
        for copy in self.copies:
            copy.start()

    def wait(self):
        for copy in self.copies:
            copy.wait()
        return self.held


def columns(ref, j):
    return ref[:, pl.ds(pl.multiple_of(j * LANES, LANES), LANES)]


def format_kernel(c_ref, send_ref, held_ref, sems, turned_ref):
    parts = sems.shape[0]
    width = c_ref.shape[1] // parts
    copies = [
        pltpu.make_async_copy(
            c_ref.at[:, part * width : (part + 1) * width],
            held_ref.at[:, part * width : (part + 1) * width],
            sems.at[part],
        )
        for part in range(parts)
    ]
    for copy in copies:
        copy.start()
    rows = held_ref.shape[0]
    for part in range(parts):
        copies[part].wait()
        for j in range(part * width // LANES, (part + 1) * width // LANES):
            lanes = slice(j * LANES, (j + 1) * LANES)
            turned_ref[lanes, 0:rows] = held_ref[:, lanes].T
    send_turned(send_ref, turned_ref)


def weights_kernel(tiles_ref, *weights_refs):
    for k, weights_ref in enumerate(weights_refs):

        def one(t, _):
            tile = tiles_ref[k, t].T
            high = tile.astype(bf16)
            low = (tile - high.astype(f32)).astype(bf16)
            lanes = pl.ds(pl.multiple_of(t * LANES, LANES), LANES)
            weights_ref[0:128, lanes] = high
            weights_ref[128:256, lanes] = high
            weights_ref[256:384, lanes] = low
            return 0

        lax.fori_loop(0, tiles_ref.shape[1], one, 0, unroll=2)


def split_all(c_ref, lhs_ref):
    def one(j, _):
        split_into(lhs_ref, j, columns(c_ref, j))
        return 0

    lax.fori_loop(0, c_ref.shape[1] // LANES, one, 0, unroll=4)


def zeros_like_block(ref):
    return lambda i: jnp.zeros(ref.shape[1:], f32)


def beta_kernel(n_ref, s_ref, c_ref, w_ref, sum_ref, *work):
    lhs_ref, products_ref, weights_ref, sem, numbers_ref, signs_ref, sems = work
    fetch = pltpu.make_async_copy(w_ref, weights_ref, sem)
    fetch.start()
    lists = Lists(0, (n_ref, s_ref), (numbers_ref, signs_ref), sems)
    split_all(c_ref, lhs_ref)
    fetch.wait()
    operate(lists, weights_ref, lhs_ref, products_ref, sum_ref, zeros_like_block(sum_ref))


def mixed_kernel(n_ref, s_ref, c_ref, w_ref, send_ref, *work):
    lhs_ref, products_ref, weights_ref, sem, numbers_ref, signs_ref, sems, sum_ref, turned_ref = work
    fetch = pltpu.make_async_copy(w_ref, weights_ref, sem)
    fetch.start()
    lists = Lists(3, (n_ref, s_ref), (numbers_ref, signs_ref), sems)
    split_all(c_ref, lhs_ref)
    fetch.wait()
    operate(lists, weights_ref, lhs_ref, products_ref, sum_ref, zeros_like_block(sum_ref))
    send_transposed(lambda j: sum_ref[j], sum_ref.shape[0], send_ref, turned_ref)


def alpha_kernel(n_ref, s_ref, recv_ref, w_ref, sum_ref, *work):
    lhs_ref, products_ref, weights_ref, sem, numbers_ref, signs_ref, sems, pieces_ref = work
    fetch = pltpu.make_async_copy(w_ref, weights_ref, sem)
    fetch.start()
    lists = Lists(1, (n_ref, s_ref), (numbers_ref, signs_ref), sems)
    receive_rows(recv_ref, pieces_ref, lhs_ref)
    fetch.wait()
    operate(lists, weights_ref, lhs_ref, products_ref, sum_ref, zeros_like_block(sum_ref))


def cross_kernel(n_ref, s_ref, recv_ref, w_ref, alpha_ref, send_ref, *work):
    lhs_ref, products_ref, weights_ref, sem, numbers_ref, signs_ref, sems, *rest = work
    pieces_ref, sum_ref, own_ref, own_sem = rest
    fetch = pltpu.make_async_copy(w_ref, weights_ref, sem)
    fetch.start()
    fetch_own = pltpu.make_async_copy(alpha_ref, own_ref, own_sem)
    fetch_own.start()
    lists = Lists(2, (n_ref, s_ref), (numbers_ref, signs_ref), sems)
    receive_rows(recv_ref, pieces_ref, lhs_ref)
    fetch.wait()
    fetch_own.wait()
    operate(lists, weights_ref, lhs_ref, products_ref, sum_ref, lambda i: own_ref[i])
    send_rows(sum_ref, send_ref)


def final_kernel(recv_ref, b_ref, o_ref, turned_ref, beta_ref, sem, out_ref, sems):
    rows = out_ref.shape[0]
    fetch = pltpu.make_async_copy(b_ref, beta_ref, sem)
    fetch.start()

    def one(d, _):
        turned_ref[pl.ds(pl.multiple_of(d * rows, 8), rows), :] = get(recv_ref, d)
        return 0

    lax.fori_loop(0, recv_ref.shape[0] // PACKED, one, 0, unroll=8)
    fetch.wait()
    parts = sems.shape[0]
    width = out_ref.shape[1] // parts
    copies = []
    for part in range(parts):
        for j in range(part * width // LANES, (part + 1) * width // LANES):
            lanes = slice(j * LANES, (j + 1) * LANES)
            out_ref[:, lanes] = turned_ref[lanes, :].T[0:rows] + beta_ref[j]
        at = slice(part * width, (part + 1) * width)
        copies.append(pltpu.make_async_copy(out_ref.at[:, at], o_ref.at[:, at], sems.at[part]))
        copies[-1].start()
    for copy in copies:
        copy.wait()


def call(kernel, out, scratch, operands, flops, held=(), out_space=VMEM, room=52):
    specs = [
        pl.BlockSpec(memory_space=VMEM if at in held else pl.ANY) for at, x in enumerate(operands)
    ]
    moved = sum(x.size * x.dtype.itemsize for x in operands)
    return pl.pallas_call(
        kernel,
        out_shape=out,
        in_specs=specs,
        out_specs=jax.tree.map(lambda _: pl.BlockSpec(memory_space=out_space), out),
        scratch_shapes=scratch,
        compiler_params=pltpu.CompilerParams(vmem_limit_bytes=room << 20),
        cost_estimate=pl.CostEstimate(flops=flops, bytes_accessed=moved, transcendentals=0),
    )(*operands)


def steps(coefficients, block_codes, tile_bank):
    shards = lax.axis_size("rows")
    irreps = lax.axis_size("irrep")
    own, codes, tiles = coefficients[0], block_codes[0], tile_bank[0]
    rows, width = own.shape
    blocks, tile_count = width // LANES, tiles.shape[1]
    flops = 6 * rows * blocks * LANES * LANES * tile_count

    packed = jax.ShapeDtypeStruct((shards * PACKED, LANES), f32)
    summed = jax.ShapeDtypeStruct((blocks, rows, LANES), f32)
    weights = jax.ShapeDtypeStruct((3 * LANES, tile_count * LANES), bf16)
    numbers, signs = runs_of(codes, blocks, tile_count)
    turned = VMEM((width, LANES), f32)
    pieces = VMEM((GROUP, rows, LANES), f32)
    total = VMEM((blocks, rows, LANES), f32)
    whole = VMEM((rows, width), f32)
    dma = pltpu.SemaphoreType.DMA
    parts = 5
    work = [
        VMEM((blocks * rows, 3 * LANES), bf16),
        VMEM((blocks * tile_count, rows, LANES), f32),
        VMEM(weights.shape, bf16),
        dma,
        SMEM(numbers.shape[1:], jnp.int32),
        SMEM(signs.shape[1:], f32),
        dma((2,)),
    ]

    def exchange(x):
        x = x.reshape(shards, PACKED // 2, 2, LANES)
        x = lax.all_to_all(x, "rows", split_axis=0, concat_axis=0, tiled=True)
        return x.reshape(shards * PACKED, LANES)

    partner = lax.ppermute(own, "irrep", [(i, i ^ irreps // 2) for i in range(irreps)])
    formatted = call(
        format_kernel, packed, [whole, dma((parts,)), turned], (own,), 1 << 20, room=60
    )
    columns_in = exchange(formatted)
    w0, w1, w2, w3 = call(weights_kernel, [weights] * tiles.shape[0], [], (tiles,), 1 << 20, (0,))
    lists = (numbers, signs)
    mixed = call(mixed_kernel, packed, [*work, total, turned], (*lists, partner, w3), flops, (2,))
    cross_in = exchange(mixed)
    beta = call(beta_kernel, summed, work, (*lists, own, w0), flops, (2,))
    alpha = call(alpha_kernel, summed, [*work, pieces], (*lists, columns_in, w1), flops, (2,))
    cross = call(
        cross_kernel,
        packed,
        [*work, pieces, total, total, dma],
        (*lists, cross_in, w2, alpha),
        flops,
        (2,),
    )
    returned = exchange(cross)
    out = call(
        final_kernel,
        jax.ShapeDtypeStruct((rows, width), f32),
        [turned, total, dma, whole, dma((parts,))],
        (returned, beta),
        1 << 20,
        (0,),
        pl.ANY,
    )
    return out[None]


def solution(mesh):
    in_specs = (
        P("irrep", "rows", None),
        P("irrep", None, None, None),
        P("irrep", None, None, None, None),
    )
    out_specs = P("irrep", "rows", None)
    return jax.shard_map(steps, mesh=mesh, in_specs=in_specs, out_specs=out_specs, check_vma=False)
```

time: 111 us -> 108 us (0.973)
  Pallas kernels: 44.1 us -> 39.4 us
  waiting for transfers between devices: 35.3 us -> 37.4 us
    pallas_call x7, Pallas kernels: 44.1 us -> 39.4 us  [call(): pl.pallas_call(kernel, out_shape=out, in_specs=specs, out_specs=jax.tree....]
    all_to_all x3, waiting for transfers between devices: 35.3 us -> 37.3 us  [exchange(): x = lax.all_to_all(x, 'rows', split_axis=0, concat_axis=0, tiled=True)]
    unnamed x14 -> x12, local copies, waits for them, and re-layouts: 3.23 us -> 2.13 us
  transfers between devices with their start and end apart: 4 -> 4, of which waited for: 3 -> 3; matrix products, arithmetic and copies ran while one was open for 2% -> 2% of each run, Pallas kernels for 27% -> 26%
where the time goes in v3:
time: 108 us; the launch traced here: 107 us
  Pallas kernels  39.4 us (36%)
  waiting for transfers between devices  37.4 us (35%)
  starting transfers between devices  25.9 us (24%)
  local copies, waits for them, and re-layouts  2.34 us (2%)
  other arithmetic  1.96 us (2%)
    pallas_call x7, Pallas kernels, call(): pl.pallas_call(kernel, out_shape=out, in_specs=specs, out_specs=jax.tree....  39.4 us
    all_to_all x3, waiting for transfers between devices, exchange(): x = lax.all_to_all(x, 'rows', split_axis=0, concat_axis=0, tiled=True)  37.3 us
    all_to_all x3, starting transfers between devices, exchange(): x = lax.all_to_all(x, 'rows', split_axis=0, concat_axis=0, tiled=True)  22.9 us
    ppermute x1, starting transfers between devices, steps(): lax.ppermute(own, 'irrep', [(i, i ^ irreps // 2) for i in range(irreps)])  3.02 us
  transfers between devices with their start and end apart: 4, of which 3 were waited for; matrix products, arithmetic and copies ran while one was open for 2% of the time, Pallas kernels for 26%

profile of v3, /device:TPU:8, one launch (start us, length us, event | category | flops | bytes accessed | tf_op | source)
XLA Modules:
  0.0 107.1 jit_solution(7140271339396007032)
XLA Ops:
  0.0 0.0 copy-start.4
  0.0 3.0 %collective-permute-start = (f32[80,2560]{1,0:T(8,128)}, f32[80,2560]{1,0:T(8,128)}, u32[]{:S(2)}, u32[]{:S(2)}) collective-permute-start(f32[80,2560]{1,0:T(8,128)} %bitcast.21), channel_id=1, source_target_pairs={{0,4},{1,5},{2,6},{3,7},{4,0},{5,1},{6,2},{7,3},{8,12},{9,13},{10,... | collective-permute-start | bytes 2457608 | tf_op jit(solution)/shard_map/ppermute | solution.py:395
  3.0 3.5 %shard_map.39 = f32[1600,128]{1,0:T(8,128)} custom-call(f32[80,2560]{1,0:T(8,128)} %bitcast.22), custom_call_target="tpu_custom_call" | custom-call | flops 1048576 | bytes 819200 | tf_op jit(solution)/shard_map/pallas_call | solution.py:351
  6.5 11.7 %all-to-all-start.1 = ((f32[32,25,2,128]{3,2,1,0:T(2,128)}), f32[32,25,2,128]{3,2,1,0:T(2,128)S(1)}, u32[]{:S(2)}, u32[]{:S(2)}) async-start(f32[32,25,2,128]{3,2,1,0:T(2,128)} %bitcast.19), calls=%async_computation.1 | async-start | bytes 1638400 | tf_op jit(solution)/shard_map/all_to_all | solution.py:392
  18.3 0.0 copy-done.4
  18.3 0.4 convert_reduce_fusion.1
  18.8 0.1 select_reduce_fusion.1
  18.9 0.7 convert_reduce_fusion
  19.6 0.5 select_reduce_fusion
  20.2 0.1 rem.42
  20.3 0.1 copy.19
  20.4 0.1 copy.15
  20.5 0.1 pad_add_fusion
  20.6 4.7 %shard_map.37 = (bf16[384,1024]{1,0:T(8,128)(2,1)S(1)}, bf16[384,1024]{1,0:T(8,128)(2,1)S(1)}, bf16[384,1024]{1,0:T(8,128)(2,1)}, bf16[384,1024]{1,0:T(8,128)(2,1)}) custom-call(f32[4,8,128,128]{3,2,1,0:T(8,128)} %bitcast.20), custom_call_target="tpu_custom_call" | custom-call | flops 1048576 | bytes 2097152 | tf_op jit(solution)/shard_map/pallas_call | solution.py:351
  25.2 0.0 collective-permute-done.c_ref
  25.2 0.0 copy-start.1
  25.2 1.1 %copy-done.1 = bf16[384,1024]{1,0:T(8,128)(2,1)S(1)} copy-done((bf16[384,1024]{1,0:T(8,128)(2,1)S(1)}, bf16[384,1024]{1,0:T(8,128)(2,1)}, u32[]{:S(2)}) %copy-start.1) | copy-done | bytes 786456
  26.4 8.1 %shard_map.38 = f32[1600,128]{1,0:T(8,128)} custom-call(s32[4,640]{1,0:T(4,128)S(1)} %pad.4.n_ref, f32[4,512]{1,0:T(4,128)S(1)} %get-tuple-element.17.s_ref, f32[80,2560]{1,0:T(8,128)} %collective-permute-done.c_ref, bf16[384,1024]{1,0:T(8,128)(2,1)S(1)} %copy-done.1), custom_call_target="tpu_custom_call" | custom-call | flops 1258291200 | bytes 1624064 | tf_op jit(solution)/shard_map/pallas_call | solution.py:351
  34.4 6.6 %all-to-all-done.1 = f32[32,25,2,128]{3,2,1,0:T(2,128)S(1)} async-done(((f32[32,25,2,128]{3,2,1,0:T(2,128)}), f32[32,25,2,128]{3,2,1,0:T(2,128)S(1)}, u32[]{:S(2)}, u32[]{:S(2)}) %all-to-all-start.1) | async-done | bytes 819232 | tf_op jit(solution)/shard_map/all_to_all | solution.py:392
  41.1 5.6 %all-to-all-start = ((f32[32,25,2,128]{3,2,1,0:T(2,128)}), f32[32,25,2,128]{3,2,1,0:T(2,128)}, u32[]{:S(2)}, u32[]{:S(2)}) async-start(f32[32,25,2,128]{3,2,1,0:T(2,128)} %bitcast.5), calls=%async_computation | async-start | bytes 1638400 | tf_op jit(solution)/shard_map/all_to_all | solution.py:392
  46.7 0.0 copy-done.3
  46.7 0.0 copy-start
  46.7 6.4 %shard_map.40.alpha_ref = f32[20,80,128]{2,1,0:T(8,128)S(1)} custom-call(s32[4,640]{1,0:T(4,128)S(1)} %pad.4.n_ref, f32[4,512]{1,0:T(4,128)S(1)} %get-tuple-element.17.s_ref, f32[1600,128]{1,0:T(8,128)} %bitcast.24, bf16[384,1024]{1,0:T(8,128)(2,1)S(1)} %get-tuple-element.11.w_ref), custom_call_target="tpu_custom_call" | custom-call | flops 1258291200 | bytes 1624064 | tf_op jit(solution)/shard_map/pallas_call | solution.py:351
  53.2 0.0 copy-start.2
  53.2 0.9 copy-done.2
  54.1 14.7 %all-to-all-done = f32[32,25,2,128]{3,2,1,0:T(2,128)} async-done(((f32[32,25,2,128]{3,2,1,0:T(2,128)}), f32[32,25,2,128]{3,2,1,0:T(2,128)}, u32[]{:S(2)}, u32[]{:S(2)}) %all-to-all-start) | async-done | bytes 819232 | tf_op jit(solution)/shard_map/all_to_all | solution.py:392
  68.8 0.0 copy-done
  68.8 9.1 %shard_map.41 = f32[1600,128]{1,0:T(8,128)} custom-call(s32[4,640]{1,0:T(4,128)S(1)} %pad.4.n_ref, f32[4,512]{1,0:T(4,128)S(1)} %get-tuple-element.17.s_ref, f32[1600,128]{1,0:T(8,128)} %bitcast.6.recv_ref, bf16[384,1024]{1,0:T(8,128)(2,1)S(1)} %copy-done, f32[20,80,128]{2,1,0:T(8,128)} %copy-done.2), custom_call_target="tpu_custom_call" | custom-call | flops 1258291200 | bytes 2443264 | tf_op jit(solution)/shard_map/pallas_call | solution.py:351
  77.9 5.6 %all-to-all-start.2 = ((f32[32,25,2,128]{3,2,1,0:T(2,128)}), f32[32,25,2,128]{3,2,1,0:T(2,128)S(1)}, u32[]{:S(2)}, u32[]{:S(2)}) async-start(f32[32,25,2,128]{3,2,1,0:T(2,128)} %bitcast.9), calls=%async_computation.2 | async-start | bytes 1638400 | tf_op jit(solution)/shard_map/all_to_all | solution.py:392
  83.4 5.6 %shard_map.42.b_ref = f32[20,80,128]{2,1,0:T(8,128)S(1)} custom-call(s32[4,640]{1,0:T(4,128)S(1)} %pad.4.n_ref, f32[4,512]{1,0:T(4,128)S(1)} %get-tuple-element.17.s_ref, f32[80,2560]{1,0:T(8,128)} %bitcast.23, bf16[384,1024]{1,0:T(8,128)(2,1)S(1)} %get-tuple-element.12.w_ref), custom_call_target="tpu_custom_call" | custom-call | flops 1258291200 | bytes 1624064 | tf_op jit(solution)/shard_map/pallas_call | solution.py:351
  89.0 16.0 %all-to-all-done.2 = f32[32,25,2,128]{3,2,1,0:T(2,128)S(1)} async-done(((f32[32,25,2,128]{3,2,1,0:T(2,128)}), f32[32,25,2,128]{3,2,1,0:T(2,128)S(1)}, u32[]{:S(2)}, u32[]{:S(2)}) %all-to-all-start.2) | async-done | bytes 819232 | tf_op jit(solution)/shard_map/all_to_all | solution.py:392
  105.0 2.1 %shard_map.43 = f32[80,2560]{1,0:T(8,128)} custom-call(f32[1600,128]{1,0:T(8,128)S(1)} %bitcast.18, f32[20,80,128]{2,1,0:T(8,128)S(1)} %shard_map.42.b_ref), custom_call_target="tpu_custom_call" | custom-call | flops 1048576 | bytes 1638400 | tf_op jit(solution)/shard_map/pallas_call | solution.py:351
  (9 shorter events, 0.1 us)
Async XLA Ops:
  0.0 18.3 %copy-start.4 = (s32[1,4,4,320]{3,2,1,0:T(4,128)S(1)}, s32[1,4,4,320]{3,2,1,0:T(4,128)}, u32[]{:S(2)}) copy-start(s32[1,4,4,320]{3,2,1,0:T(4,128)} %param.4) | copy-start | bytes 61444
  0.0 25.2 %collective-permute-start = (f32[80,2560]{1,0:T(8,128)}, f32[80,2560]{1,0:T(8,128)}, u32[]{:S(2)}, u32[]{:S(2)}) collective-permute-start(f32[80,2560]{1,0:T(8,128)} %bitcast.21), channel_id=1, source_target_pairs={{0,4},{1,5},{2,6},{3,7},{4,0},{5,1},{6,2},{7,3},{8,12},{9,13},{10,... | collective-permute-start | bytes 2457608 | tf_op jit(solution)/shard_map/ppermute | solution.py:395
  6.5 34.6 %all-to-all-start.1 = ((f32[32,25,2,128]{3,2,1,0:T(2,128)}), f32[32,25,2,128]{3,2,1,0:T(2,128)S(1)}, u32[]{:S(2)}, u32[]{:S(2)}) async-start(f32[32,25,2,128]{3,2,1,0:T(2,128)} %bitcast.19), calls=%async_computation.1 | async-start | bytes 1638400 | tf_op jit(solution)/shard_map/all_to_all | solution.py:392
  25.2 1.1 %copy-start.1 = (bf16[384,1024]{1,0:T(8,128)(2,1)S(1)}, bf16[384,1024]{1,0:T(8,128)(2,1)}, u32[]{:S(2)}) copy-start(bf16[384,1024]{1,0:T(8,128)(2,1)} %get-tuple-element.9.w_ref) | copy-start | bytes 2359300
  41.1 5.6 %copy-start.3 = (f32[32,25,2,128]{3,2,1,0:T(2,128)}, f32[32,25,2,128]{3,2,1,0:T(2,128)S(1)}, u32[]{:S(2)}) copy-start(f32[32,25,2,128]{3,2,1,0:T(2,128)S(1)} %all-to-all-done.1) | copy-start | bytes 2457604
  41.1 27.7 %all-to-all-start = ((f32[32,25,2,128]{3,2,1,0:T(2,128)}), f32[32,25,2,128]{3,2,1,0:T(2,128)}, u32[]{:S(2)}, u32[]{:S(2)}) async-start(f32[32,25,2,128]{3,2,1,0:T(2,128)} %bitcast.5), calls=%async_computation | async-start | bytes 1638400 | tf_op jit(solution)/shard_map/all_to_all | solution.py:392
  46.7 22.0 %copy-start = (bf16[384,1024]{1,0:T(8,128)(2,1)S(1)}, bf16[384,1024]{1,0:T(8,128)(2,1)}, u32[]{:S(2)}) copy-start(bf16[384,1024]{1,0:T(8,128)(2,1)} %get-tuple-element.10.w_ref) | copy-start | bytes 2359300
  53.2 0.9 copy-start.2
  77.9 27.2 %all-to-all-start.2 = ((f32[32,25,2,128]{3,2,1,0:T(2,128)}), f32[32,25,2,128]{3,2,1,0:T(2,128)S(1)}, u32[]{:S(2)}, u32[]{:S(2)}) async-start(f32[32,25,2,128]{3,2,1,0:T(2,128)} %bitcast.9), calls=%async_computation.2 | async-start | bytes 1638400 | tf_op jit(solution)/shard_map/all_to_all | solution.py:392

commit v4 on v3

--- a/solution.py
+++ b/solution.py
@@ -67,26 +67,38 @@
     return jnp.concatenate([p[0:48], rows48, *last], axis=0)
 
 
-def send_transposed(tile_at, count, send_ref, turned_ref):
-    rows = turned_ref.shape[0] * PACKED // send_ref.shape[0]
+def send_transposed(tile_at, count, out, turned_ref):
+    rows = turned_ref.shape[0] * PACKED // out[1].shape[0]
 
     def turn(j, _):
         turned_ref[pl.ds(pl.multiple_of(j * LANES, LANES), LANES), 0:rows] = tile_at(j).T
         return 0
 
-    lax.fori_loop(0, count, turn, 0, unroll=5)
-    send_turned(send_ref, turned_ref)
-
-
-def send_turned(send_ref, turned_ref):
+    lax.fori_loop(0, count, turn, 0, unroll=10)
+    send_turned(out, turned_ref)
+
+
+def send_turned(out, turned_ref):
+    o_ref, send_ref, sems = out
+    halves = sems.shape[0]
     shards = send_ref.shape[0] // PACKED
     rows = turned_ref.shape[0] // shards
-
-    def one(d, _):
-        put(send_ref, d, turned_ref[pl.ds(pl.multiple_of(d * rows, 8), rows), :])
-        return 0
-
-    lax.fori_loop(0, shards, one, 0, unroll=8)
+    each = shards // halves
+
+    def copy_of(h):
+        at = pl.ds(pl.multiple_of(h * each * PACKED, 8), each * PACKED)
+        return pltpu.make_async_copy(send_ref.at[at], o_ref.at[at], sems.at[h])
+
+    def half(h, _):
+        for c in range(each):
+            d = h * each + c
+            put(send_ref, d, turned_ref[pl.ds(pl.multiple_of(d * rows, 8), rows), :])
+        copy_of(h).start()
+        return 0
+
+    lax.fori_loop(0, halves, half, 0)
+    for h in range(halves):
+        copy_of(h).wait()
 
 
 def split_into(lhs_ref, j, value):
@@ -119,7 +131,7 @@
     lax.fori_loop(0, recv_ref.shape[0] // PACKED // GROUP, group, 0)
 
 
-def send_rows(sum_ref, send_ref):
+def send_rows(sum_ref, out, turned_ref):
     rows = sum_ref.shape[1]
 
     def group(g, _):
@@ -131,13 +143,14 @@
                 value = jnp.where(
                     lane_of(rows) < LANES - o, value, rolled(sum_ref[base + b + 1], -o)
                 )
-            put(send_ref, g * GROUP + c, value)
-        return 0
-
-    lax.fori_loop(0, send_ref.shape[0] // PACKED // GROUP, group, 0)
-
-
-def operate(lists, weights_ref, lhs_ref, products_ref, sum_ref, first):
+            turned_ref[pl.ds(pl.multiple_of((g * GROUP + c) * rows, 8), rows), :] = value
+        return 0
+
+    lax.fori_loop(0, turned_ref.shape[0] // rows // GROUP, group, 0)
+    send_turned(out, turned_ref)
+
+
+def operate(lists, weights_ref, lhs_ref, products_ref, sum_ref):
     blocks, rows, _ = sum_ref.shape
     tile_count = products_ref.shape[0] // blocks
     numbers_ref, signs_ref = lists.wait()
@@ -153,8 +166,6 @@
         return 0
 
     lax.fori_loop(0, tile_count // 2, multiply, 0)
-    for i in range(blocks):
-        sum_ref[i] = first(i)
     slots = signs_ref.shape[0]
 
     def run(q, _):
@@ -222,7 +233,7 @@
     return ref[:, pl.ds(pl.multiple_of(j * LANES, LANES), LANES)]
 
 
-def format_kernel(c_ref, send_ref, held_ref, sems, turned_ref):
+def format_kernel(c_ref, o_ref, held_ref, sems, turned_ref, *buffer):
     parts = sems.shape[0]
     width = c_ref.shape[1] // parts
     copies = [
@@ -241,7 +252,7 @@
         for j in range(part * width // LANES, (part + 1) * width // LANES):
             lanes = slice(j * LANES, (j + 1) * LANES)
             turned_ref[lanes, 0:rows] = held_ref[:, lanes].T
-    send_turned(send_ref, turned_ref)
+    send_turned((o_ref, *buffer), turned_ref)
 
 
 def weights_kernel(tiles_ref, *weights_refs):
@@ -268,10 +279,6 @@
     lax.fori_loop(0, c_ref.shape[1] // LANES, one, 0, unroll=4)
 
 
-def zeros_like_block(ref):
-    return lambda i: jnp.zeros(ref.shape[1:], f32)
-
-
 def beta_kernel(n_ref, s_ref, c_ref, w_ref, sum_ref, *work):
     lhs_ref, products_ref, weights_ref, sem, numbers_ref, signs_ref, sems = work
     fetch = pltpu.make_async_copy(w_ref, weights_ref, sem)
@@ -279,18 +286,21 @@
     lists = Lists(0, (n_ref, s_ref), (numbers_ref, signs_ref), sems)
     split_all(c_ref, lhs_ref)
     fetch.wait()
-    operate(lists, weights_ref, lhs_ref, products_ref, sum_ref, zeros_like_block(sum_ref))
-
-
-def mixed_kernel(n_ref, s_ref, c_ref, w_ref, send_ref, *work):
-    lhs_ref, products_ref, weights_ref, sem, numbers_ref, signs_ref, sems, sum_ref, turned_ref = work
+    sum_ref[...] = jnp.zeros_like(sum_ref)
+    operate(lists, weights_ref, lhs_ref, products_ref, sum_ref)
+
+
+def mixed_kernel(n_ref, s_ref, c_ref, w_ref, o_ref, *work):
+    lhs_ref, products_ref, weights_ref, sem, numbers_ref, signs_ref, sems, *rest = work
+    sum_ref, turned_ref, *buffer = rest
     fetch = pltpu.make_async_copy(w_ref, weights_ref, sem)
     fetch.start()
     lists = Lists(3, (n_ref, s_ref), (numbers_ref, signs_ref), sems)
     split_all(c_ref, lhs_ref)
     fetch.wait()
-    operate(lists, weights_ref, lhs_ref, products_ref, sum_ref, zeros_like_block(sum_ref))
-    send_transposed(lambda j: sum_ref[j], sum_ref.shape[0], send_ref, turned_ref)
+    sum_ref[...] = jnp.zeros_like(sum_ref)
+    operate(lists, weights_ref, lhs_ref, products_ref, sum_ref)
+    send_transposed(lambda j: sum_ref[j], sum_ref.shape[0], (o_ref, *buffer), turned_ref)
 
 
 def alpha_kernel(n_ref, s_ref, recv_ref, w_ref, sum_ref, *work):
@@ -300,22 +310,23 @@
     lists = Lists(1, (n_ref, s_ref), (numbers_ref, signs_ref), sems)
     receive_rows(recv_ref, pieces_ref, lhs_ref)
     fetch.wait()
-    operate(lists, weights_ref, lhs_ref, products_ref, sum_ref, zeros_like_block(sum_ref))
-
-
-def cross_kernel(n_ref, s_ref, recv_ref, w_ref, alpha_ref, send_ref, *work):
+    sum_ref[...] = jnp.zeros_like(sum_ref)
+    operate(lists, weights_ref, lhs_ref, products_ref, sum_ref)
+
+
+def cross_kernel(n_ref, s_ref, recv_ref, w_ref, alpha_ref, o_ref, *work):
     lhs_ref, products_ref, weights_ref, sem, numbers_ref, signs_ref, sems, *rest = work
-    pieces_ref, sum_ref, own_ref, own_sem = rest
+    pieces_ref, sum_ref, own_sem, turned_ref, *buffer = rest
     fetch = pltpu.make_async_copy(w_ref, weights_ref, sem)
     fetch.start()
-    fetch_own = pltpu.make_async_copy(alpha_ref, own_ref, own_sem)
+    fetch_own = pltpu.make_async_copy(alpha_ref, sum_ref, own_sem)
     fetch_own.start()
     lists = Lists(2, (n_ref, s_ref), (numbers_ref, signs_ref), sems)
     receive_rows(recv_ref, pieces_ref, lhs_ref)
     fetch.wait()
     fetch_own.wait()
-    operate(lists, weights_ref, lhs_ref, products_ref, sum_ref, lambda i: own_ref[i])
-    send_rows(sum_ref, send_ref)
+    operate(lists, weights_ref, lhs_ref, products_ref, sum_ref)
+    send_rows(sum_ref, (o_ref, *buffer), turned_ref)
 
 
 def final_kernel(recv_ref, b_ref, o_ref, turned_ref, beta_ref, sem, out_ref, sems):
@@ -327,7 +338,7 @@
         turned_ref[pl.ds(pl.multiple_of(d * rows, 8), rows), :] = get(recv_ref, d)
         return 0
 
-    lax.fori_loop(0, recv_ref.shape[0] // PACKED, one, 0, unroll=8)
+    lax.fori_loop(0, recv_ref.shape[0] // PACKED, one, 0, unroll=16)
     fetch.wait()
     parts = sems.shape[0]
     width = out_ref.shape[1] // parts
@@ -377,6 +388,7 @@
     whole = VMEM((rows, width), f32)
     dma = pltpu.SemaphoreType.DMA
     parts = 5
+    buffer = [VMEM(packed.shape, f32), dma((2,))]
     work = [
         VMEM((blocks * rows, 3 * LANES), bf16),
         VMEM((blocks * tile_count, rows, LANES), f32),
@@ -394,22 +406,37 @@
 
     partner = lax.ppermute(own, "irrep", [(i, i ^ irreps // 2) for i in range(irreps)])
     formatted = call(
-        format_kernel, packed, [whole, dma((parts,)), turned], (own,), 1 << 20, room=60
+        format_kernel,
+        packed,
+        [whole, dma((parts,)), turned, *buffer],
+        (own,),
+        1 << 20,
+        out_space=pl.ANY,
+        room=60,
     )
     columns_in = exchange(formatted)
     w0, w1, w2, w3 = call(weights_kernel, [weights] * tiles.shape[0], [], (tiles,), 1 << 20, (0,))
     lists = (numbers, signs)
-    mixed = call(mixed_kernel, packed, [*work, total, turned], (*lists, partner, w3), flops, (2,))
+    mixed = call(
+        mixed_kernel,
+        packed,
+        [*work, total, turned, *buffer],
+        (*lists, partner, w3),
+        flops,
+        (2,),
+        pl.ANY,
+    )
     cross_in = exchange(mixed)
     beta = call(beta_kernel, summed, work, (*lists, own, w0), flops, (2,))
     alpha = call(alpha_kernel, summed, [*work, pieces], (*lists, columns_in, w1), flops, (2,))
     cross = call(
         cross_kernel,
         packed,
-        [*work, pieces, total, total, dma],
+        [*work, pieces, total, dma, turned, *buffer],
         (*lists, cross_in, w2, alpha),
         flops,
         (2,),
+        pl.ANY,
     )
     returned = exchange(cross)
     out = call(

time: 108 us -> 107 us (level)
  Pallas kernels: 39.4 us -> 37.9 us
    pallas_call x7, Pallas kernels: 39.4 us -> 37.9 us  [call(): pl.pallas_call(kernel, out_shape=out, in_specs=specs, out_specs=jax.tree....]
where the time goes in v4:
time: 107 us; the launch traced here: 106 us
  Pallas kernels  37.9 us (35%)
  waiting for transfers between devices  37.9 us (35%)
  starting transfers between devices  25.9 us (24%)
  local copies, waits for them, and re-layouts  2.34 us (2%)
  other arithmetic  1.96 us (2%)
    all_to_all x3, waiting for transfers between devices, exchange(): x = lax.all_to_all(x, 'rows', split_axis=0, concat_axis=0, tiled=True)  37.9 us
    pallas_call x7, Pallas kernels, call(): pl.pallas_call(kernel, out_shape=out, in_specs=specs, out_specs=jax.tree....  37.9 us
    all_to_all x3, starting transfers between devices, exchange(): x = lax.all_to_all(x, 'rows', split_axis=0, concat_axis=0, tiled=True)  22.9 us
    ppermute x1, starting transfers between devices, steps(): lax.ppermute(own, 'irrep', [(i, i ^ irreps // 2) for i in range(irreps)])  3.02 us
  transfers between devices with their start and end apart: 4, of which 3 were waited for; matrix products, arithmetic and copies ran while one was open for 2% of the time, Pallas kernels for 26%

profile of v4, /device:TPU:8, one launch (start us, length us, event | category | flops | bytes accessed | tf_op | source)
XLA Modules:
  0.0 106.2 jit_solution(13281801587691362886)
XLA Ops:
  0.0 0.0 copy-start.4
  0.0 3.0 %collective-permute-start = (f32[80,2560]{1,0:T(8,128)}, f32[80,2560]{1,0:T(8,128)}, u32[]{:S(2)}, u32[]{:S(2)}) collective-permute-start(f32[80,2560]{1,0:T(8,128)} %bitcast.21), channel_id=1, source_target_pairs={{0,4},{1,5},{2,6},{3,7},{4,0},{5,1},{6,2},{7,3},{8,12},{9,13},{10,... | collective-permute-start | bytes 2457608 | tf_op jit(solution)/shard_map/ppermute | solution.py:407
  3.0 3.1 %shard_map.39 = f32[1600,128]{1,0:T(8,128)} custom-call(f32[80,2560]{1,0:T(8,128)} %bitcast.22), custom_call_target="tpu_custom_call" | custom-call | flops 1048576 | bytes 819200 | tf_op jit(solution)/shard_map/pallas_call | solution.py:362
  6.2 11.7 %all-to-all-start.1 = ((f32[32,25,2,128]{3,2,1,0:T(2,128)}), f32[32,25,2,128]{3,2,1,0:T(2,128)S(1)}, u32[]{:S(2)}, u32[]{:S(2)}) async-start(f32[32,25,2,128]{3,2,1,0:T(2,128)} %bitcast.19), calls=%async_computation.1 | async-start | bytes 1638400 | tf_op jit(solution)/shard_map/all_to_all | solution.py:404
  17.9 0.0 copy-done.4
  18.0 0.4 convert_reduce_fusion.1
  18.4 0.1 select_reduce_fusion.1
  18.6 0.7 convert_reduce_fusion
  19.3 0.5 select_reduce_fusion
  19.8 0.1 rem.42
  20.0 0.1 copy.19
  20.0 0.1 copy.15
  20.1 0.1 pad_add_fusion
  20.2 4.7 %shard_map.37 = (bf16[384,1024]{1,0:T(8,128)(2,1)S(1)}, bf16[384,1024]{1,0:T(8,128)(2,1)S(1)}, bf16[384,1024]{1,0:T(8,128)(2,1)}, bf16[384,1024]{1,0:T(8,128)(2,1)}) custom-call(f32[4,8,128,128]{3,2,1,0:T(8,128)} %bitcast.20), custom_call_target="tpu_custom_call" | custom-call | flops 1048576 | bytes 2097152 | tf_op jit(solution)/shard_map/pallas_call | solution.py:362
  24.9 0.0 collective-permute-done.c_ref
  24.9 0.0 copy-start.1
  24.9 1.1 %copy-done.1 = bf16[384,1024]{1,0:T(8,128)(2,1)S(1)} copy-done((bf16[384,1024]{1,0:T(8,128)(2,1)S(1)}, bf16[384,1024]{1,0:T(8,128)(2,1)}, u32[]{:S(2)}) %copy-start.1) | copy-done | bytes 786456
  26.0 7.5 %shard_map.38 = f32[1600,128]{1,0:T(8,128)} custom-call(s32[4,640]{1,0:T(4,128)S(1)} %pad.4.n_ref, f32[4,512]{1,0:T(4,128)S(1)} %get-tuple-element.17.s_ref, f32[80,2560]{1,0:T(8,128)} %collective-permute-done.c_ref, bf16[384,1024]{1,0:T(8,128)(2,1)S(1)} %copy-done.1), custom_call_target="tpu_custom_call" | custom-call | flops 1258291200 | bytes 1624064 | tf_op jit(solution)/shard_map/pallas_call | solution.py:362
  33.6 7.2 %all-to-all-done.1 = f32[32,25,2,128]{3,2,1,0:T(2,128)S(1)} async-done(((f32[32,25,2,128]{3,2,1,0:T(2,128)}), f32[32,25,2,128]{3,2,1,0:T(2,128)S(1)}, u32[]{:S(2)}, u32[]{:S(2)}) %all-to-all-start.1) | async-done | bytes 819232 | tf_op jit(solution)/shard_map/all_to_all | solution.py:404
  40.8 5.6 %all-to-all-start = ((f32[32,25,2,128]{3,2,1,0:T(2,128)}), f32[32,25,2,128]{3,2,1,0:T(2,128)}, u32[]{:S(2)}, u32[]{:S(2)}) async-start(f32[32,25,2,128]{3,2,1,0:T(2,128)} %bitcast.5), calls=%async_computation | async-start | bytes 1638400 | tf_op jit(solution)/shard_map/all_to_all | solution.py:404
  46.4 0.0 copy-done.3
  46.4 0.0 copy-start
  46.4 6.5 %shard_map.40.alpha_ref = f32[20,80,128]{2,1,0:T(8,128)S(1)} custom-call(s32[4,640]{1,0:T(4,128)S(1)} %pad.4.n_ref, f32[4,512]{1,0:T(4,128)S(1)} %get-tuple-element.17.s_ref, f32[1600,128]{1,0:T(8,128)} %bitcast.24, bf16[384,1024]{1,0:T(8,128)(2,1)S(1)} %get-tuple-element.11.w_ref), custom_call_target="tpu_custom_call" | custom-call | flops 1258291200 | bytes 1624064 | tf_op jit(solution)/shard_map/pallas_call | solution.py:362
  52.9 0.0 copy-start.2
  52.9 0.9 copy-done.2
  53.8 14.7 %all-to-all-done = f32[32,25,2,128]{3,2,1,0:T(2,128)} async-done(((f32[32,25,2,128]{3,2,1,0:T(2,128)}), f32[32,25,2,128]{3,2,1,0:T(2,128)}, u32[]{:S(2)}, u32[]{:S(2)}) %all-to-all-start) | async-done | bytes 819232 | tf_op jit(solution)/shard_map/all_to_all | solution.py:404
  68.4 0.0 copy-done
  68.4 8.5 %shard_map.41 = f32[1600,128]{1,0:T(8,128)} custom-call(s32[4,640]{1,0:T(4,128)S(1)} %pad.4.n_ref, f32[4,512]{1,0:T(4,128)S(1)} %get-tuple-element.17.s_ref, f32[1600,128]{1,0:T(8,128)} %bitcast.6.recv_ref, bf16[384,1024]{1,0:T(8,128)(2,1)S(1)} %copy-done, f32[20,80,128]{2,1,0:T(8,128)} %copy-done.2), custom_call_target="tpu_custom_call" | custom-call | flops 1258291200 | bytes 2443264 | tf_op jit(solution)/shard_map/pallas_call | solution.py:362
  77.0 5.6 %all-to-all-start.2 = ((f32[32,25,2,128]{3,2,1,0:T(2,128)}), f32[32,25,2,128]{3,2,1,0:T(2,128)S(1)}, u32[]{:S(2)}, u32[]{:S(2)}) async-start(f32[32,25,2,128]{3,2,1,0:T(2,128)} %bitcast.9), calls=%async_computation.2 | async-start | bytes 1638400 | tf_op jit(solution)/shard_map/all_to_all | solution.py:404
  82.6 5.5 %shard_map.42.b_ref = f32[20,80,128]{2,1,0:T(8,128)S(1)} custom-call(s32[4,640]{1,0:T(4,128)S(1)} %pad.4.n_ref, f32[4,512]{1,0:T(4,128)S(1)} %get-tuple-element.17.s_ref, f32[80,2560]{1,0:T(8,128)} %bitcast.23, bf16[384,1024]{1,0:T(8,128)(2,1)S(1)} %get-tuple-element.12.w_ref), custom_call_target="tpu_custom_call" | custom-call | flops 1258291200 | bytes 1624064 | tf_op jit(solution)/shard_map/pallas_call | solution.py:362
  88.1 16.1 %all-to-all-done.2 = f32[32,25,2,128]{3,2,1,0:T(2,128)S(1)} async-done(((f32[32,25,2,128]{3,2,1,0:T(2,128)}), f32[32,25,2,128]{3,2,1,0:T(2,128)S(1)}, u32[]{:S(2)}, u32[]{:S(2)}) %all-to-all-start.2) | async-done | bytes 819232 | tf_op jit(solution)/shard_map/all_to_all | solution.py:404
  104.2 2.0 %shard_map.43 = f32[80,2560]{1,0:T(8,128)} custom-call(f32[1600,128]{1,0:T(8,128)S(1)} %bitcast.18, f32[20,80,128]{2,1,0:T(8,128)S(1)} %shard_map.42.b_ref), custom_call_target="tpu_custom_call" | custom-call | flops 1048576 | bytes 1638400 | tf_op jit(solution)/shard_map/pallas_call | solution.py:362
  (9 shorter events, 0.1 us)
Async XLA Ops:
  0.0 17.9 %copy-start.4 = (s32[1,4,4,320]{3,2,1,0:T(4,128)S(1)}, s32[1,4,4,320]{3,2,1,0:T(4,128)}, u32[]{:S(2)}) copy-start(s32[1,4,4,320]{3,2,1,0:T(4,128)} %param.4) | copy-start | bytes 61444
  0.0 24.9 %collective-permute-start = (f32[80,2560]{1,0:T(8,128)}, f32[80,2560]{1,0:T(8,128)}, u32[]{:S(2)}, u32[]{:S(2)}) collective-permute-start(f32[80,2560]{1,0:T(8,128)} %bitcast.21), channel_id=1, source_target_pairs={{0,4},{1,5},{2,6},{3,7},{4,0},{5,1},{6,2},{7,3},{8,12},{9,13},{10,... | collective-permute-start | bytes 2457608 | tf_op jit(solution)/shard_map/ppermute | solution.py:407
  6.2 34.6 %all-to-all-start.1 = ((f32[32,25,2,128]{3,2,1,0:T(2,128)}), f32[32,25,2,128]{3,2,1,0:T(2,128)S(1)}, u32[]{:S(2)}, u32[]{:S(2)}) async-start(f32[32,25,2,128]{3,2,1,0:T(2,128)} %bitcast.19), calls=%async_computation.1 | async-start | bytes 1638400 | tf_op jit(solution)/shard_map/all_to_all | solution.py:404
  24.9 1.1 %copy-start.1 = (bf16[384,1024]{1,0:T(8,128)(2,1)S(1)}, bf16[384,1024]{1,0:T(8,128)(2,1)}, u32[]{:S(2)}) copy-start(bf16[384,1024]{1,0:T(8,128)(2,1)} %get-tuple-element.9.w_ref) | copy-start | bytes 2359300
  40.8 5.6 %copy-start.3 = (f32[32,25,2,128]{3,2,1,0:T(2,128)}, f32[32,25,2,128]{3,2,1,0:T(2,128)S(1)}, u32[]{:S(2)}) copy-start(f32[32,25,2,128]{3,2,1,0:T(2,128)S(1)} %all-to-all-done.1) | copy-start | bytes 2457604
  40.8 27.7 %all-to-all-start = ((f32[32,25,2,128]{3,2,1,0:T(2,128)}), f32[32,25,2,128]{3,2,1,0:T(2,128)}, u32[]{:S(2)}, u32[]{:S(2)}) async-start(f32[32,25,2,128]{3,2,1,0:T(2,128)} %bitcast.5), calls=%async_computation | async-start | bytes 1638400 | tf_op jit(solution)/shard_map/all_to_all | solution.py:404
  46.4 22.0 %copy-start = (bf16[384,1024]{1,0:T(8,128)(2,1)S(1)}, bf16[384,1024]{1,0:T(8,128)(2,1)}, u32[]{:S(2)}) copy-start(bf16[384,1024]{1,0:T(8,128)(2,1)} %get-tuple-element.10.w_ref) | copy-start | bytes 2359300
  52.9 0.9 copy-start.2
  77.0 27.2 %all-to-all-start.2 = ((f32[32,25,2,128]{3,2,1,0:T(2,128)}), f32[32,25,2,128]{3,2,1,0:T(2,128)S(1)}, u32[]{:S(2)}, u32[]{:S(2)}) async-start(f32[32,25,2,128]{3,2,1,0:T(2,128)} %bitcast.9), calls=%async_computation.2 | async-start | bytes 1638400 | tf_op jit(solution)/shard_map/all_to_all | solution.py:404

commit v5 on v4

--- a/solution.py
+++ b/solution.py
@@ -131,7 +131,7 @@
     lax.fori_loop(0, recv_ref.shape[0] // PACKED // GROUP, group, 0)
 
 
-def send_rows(sum_ref, out, turned_ref):
+def send_rows(sum_ref, send_ref, turned_ref):
     rows = sum_ref.shape[1]
 
     def group(g, _):
@@ -147,7 +147,12 @@
         return 0
 
     lax.fori_loop(0, turned_ref.shape[0] // rows // GROUP, group, 0)
-    send_turned(out, turned_ref)
+
+    def one(d, _):
+        put(send_ref, d, turned_ref[pl.ds(pl.multiple_of(d * rows, 8), rows), :])
+        return 0
+
+    lax.fori_loop(0, send_ref.shape[0] // PACKED, one, 0, unroll=16)
 
 
 def operate(lists, weights_ref, lhs_ref, products_ref, sum_ref):
@@ -314,9 +319,9 @@
     operate(lists, weights_ref, lhs_ref, products_ref, sum_ref)
 
 
-def cross_kernel(n_ref, s_ref, recv_ref, w_ref, alpha_ref, o_ref, *work):
+def cross_kernel(n_ref, s_ref, recv_ref, w_ref, alpha_ref, send_ref, *work):
     lhs_ref, products_ref, weights_ref, sem, numbers_ref, signs_ref, sems, *rest = work
-    pieces_ref, sum_ref, own_sem, turned_ref, *buffer = rest
+    pieces_ref, sum_ref, own_sem, turned_ref = rest
     fetch = pltpu.make_async_copy(w_ref, weights_ref, sem)
     fetch.start()
     fetch_own = pltpu.make_async_copy(alpha_ref, sum_ref, own_sem)
@@ -326,7 +331,7 @@
     fetch.wait()
     fetch_own.wait()
     operate(lists, weights_ref, lhs_ref, products_ref, sum_ref)
-    send_rows(sum_ref, (o_ref, *buffer), turned_ref)
+    send_rows(sum_ref, send_ref, turned_ref)
 
 
 def final_kernel(recv_ref, b_ref, o_ref, turned_ref, beta_ref, sem, out_ref, sems):
@@ -432,11 +437,10 @@
     cross = call(
         cross_kernel,
         packed,
-        [*work, pieces, total, dma, turned, *buffer],
+        [*work, pieces, total, dma, turned],
         (*lists, cross_in, w2, alpha),
         flops,
         (2,),
-        pl.ANY,
     )
     returned = exchange(cross)
     out = call(

time: 107 us -> 107 us (level)
  no operation moved by 1% of the time
where the time goes in v5:
time: 107 us; the launch traced here: 106 us
  Pallas kernels  38 us (36%)
  waiting for transfers between devices  37.9 us (35%)
  starting transfers between devices  25.9 us (24%)
  local copies, waits for them, and re-layouts  2.34 us (2%)
  other arithmetic  1.96 us (2%)
    pallas_call x7, Pallas kernels, call(): pl.pallas_call(kernel, out_shape=out, in_specs=specs, out_specs=jax.tree....  38 us
    all_to_all x3, waiting for transfers between devices, exchange(): x = lax.all_to_all(x, 'rows', split_axis=0, concat_axis=0, tiled=True)  37.9 us
    all_to_all x3, starting transfers between devices, exchange(): x = lax.all_to_all(x, 'rows', split_axis=0, concat_axis=0, tiled=True)  22.9 us
    ppermute x1, starting transfers between devices, steps(): lax.ppermute(own, 'irrep', [(i, i ^ irreps // 2) for i in range(irreps)])  3.02 us
  transfers between devices with their start and end apart: 4, of which 3 were waited for; matrix products, arithmetic and copies ran while one was open for 2% of the time, Pallas kernels for 26%

profile of v5, /device:TPU:8, one launch (start us, length us, event | category | flops | bytes accessed | tf_op | source)
XLA Modules:
  0.0 106.3 jit_solution(8283995734432260947)
XLA Ops:
  0.0 0.0 copy-start.4
  0.0 3.0 %collective-permute-start = (f32[80,2560]{1,0:T(8,128)}, f32[80,2560]{1,0:T(8,128)}, u32[]{:S(2)}, u32[]{:S(2)}) collective-permute-start(f32[80,2560]{1,0:T(8,128)} %bitcast.21), channel_id=1, source_target_pairs={{0,4},{1,5},{2,6},{3,7},{4,0},{5,1},{6,2},{7,3},{8,12},{9,13},{10,... | collective-permute-start | bytes 2457608 | tf_op jit(solution)/shard_map/ppermute | solution.py:412
  3.0 3.1 %shard_map.39 = f32[1600,128]{1,0:T(8,128)} custom-call(f32[80,2560]{1,0:T(8,128)} %bitcast.22), custom_call_target="tpu_custom_call" | custom-call | flops 1048576 | bytes 819200 | tf_op jit(solution)/shard_map/pallas_call | solution.py:367
  6.2 11.7 %all-to-all-start.1 = ((f32[32,25,2,128]{3,2,1,0:T(2,128)}), f32[32,25,2,128]{3,2,1,0:T(2,128)S(1)}, u32[]{:S(2)}, u32[]{:S(2)}) async-start(f32[32,25,2,128]{3,2,1,0:T(2,128)} %bitcast.19), calls=%async_computation.1 | async-start | bytes 1638400 | tf_op jit(solution)/shard_map/all_to_all | solution.py:409
  17.9 0.0 copy-done.4
  18.0 0.4 convert_reduce_fusion.1
  18.4 0.1 select_reduce_fusion.1
  18.6 0.7 convert_reduce_fusion
  19.3 0.5 select_reduce_fusion
  19.8 0.1 rem.42
  20.0 0.1 copy.19
  20.0 0.1 copy.15
  20.1 0.1 pad_add_fusion
  20.2 4.7 %shard_map.37 = (bf16[384,1024]{1,0:T(8,128)(2,1)S(1)}, bf16[384,1024]{1,0:T(8,128)(2,1)S(1)}, bf16[384,1024]{1,0:T(8,128)(2,1)}, bf16[384,1024]{1,0:T(8,128)(2,1)}) custom-call(f32[4,8,128,128]{3,2,1,0:T(8,128)} %bitcast.20), custom_call_target="tpu_custom_call" | custom-call | flops 1048576 | bytes 2097152 | tf_op jit(solution)/shard_map/pallas_call | solution.py:367
  24.9 0.0 collective-permute-done.c_ref
  24.9 0.0 copy-start.1
  24.9 1.1 %copy-done.1 = bf16[384,1024]{1,0:T(8,128)(2,1)S(1)} copy-done((bf16[384,1024]{1,0:T(8,128)(2,1)S(1)}, bf16[384,1024]{1,0:T(8,128)(2,1)}, u32[]{:S(2)}) %copy-start.1) | copy-done | bytes 786456
  26.0 7.5 %shard_map.38 = f32[1600,128]{1,0:T(8,128)} custom-call(s32[4,640]{1,0:T(4,128)S(1)} %pad.4.n_ref, f32[4,512]{1,0:T(4,128)S(1)} %get-tuple-element.17.s_ref, f32[80,2560]{1,0:T(8,128)} %collective-permute-done.c_ref, bf16[384,1024]{1,0:T(8,128)(2,1)S(1)} %copy-done.1), custom_call_target="tpu_custom_call" | custom-call | flops 1258291200 | bytes 1624064 | tf_op jit(solution)/shard_map/pallas_call | solution.py:367
  33.6 7.2 %all-to-all-done.1 = f32[32,25,2,128]{3,2,1,0:T(2,128)S(1)} async-done(((f32[32,25,2,128]{3,2,1,0:T(2,128)}), f32[32,25,2,128]{3,2,1,0:T(2,128)S(1)}, u32[]{:S(2)}, u32[]{:S(2)}) %all-to-all-start.1) | async-done | bytes 819232 | tf_op jit(solution)/shard_map/all_to_all | solution.py:409
  40.8 5.6 %all-to-all-start = ((f32[32,25,2,128]{3,2,1,0:T(2,128)}), f32[32,25,2,128]{3,2,1,0:T(2,128)}, u32[]{:S(2)}, u32[]{:S(2)}) async-start(f32[32,25,2,128]{3,2,1,0:T(2,128)} %bitcast.5), calls=%async_computation | async-start | bytes 1638400 | tf_op jit(solution)/shard_map/all_to_all | solution.py:409
  46.4 0.0 copy-done.3
  46.4 0.0 copy-start
  46.4 6.5 %shard_map.40.alpha_ref = f32[20,80,128]{2,1,0:T(8,128)S(1)} custom-call(s32[4,640]{1,0:T(4,128)S(1)} %pad.4.n_ref, f32[4,512]{1,0:T(4,128)S(1)} %get-tuple-element.17.s_ref, f32[1600,128]{1,0:T(8,128)} %bitcast.24, bf16[384,1024]{1,0:T(8,128)(2,1)S(1)} %get-tuple-element.11.w_ref), custom_call_target="tpu_custom_call" | custom-call | flops 1258291200 | bytes 1624064 | tf_op jit(solution)/shard_map/pallas_call | solution.py:367
  52.9 0.0 copy-start.2
  52.9 0.9 copy-done.2
  53.8 14.7 %all-to-all-done = f32[32,25,2,128]{3,2,1,0:T(2,128)} async-done(((f32[32,25,2,128]{3,2,1,0:T(2,128)}), f32[32,25,2,128]{3,2,1,0:T(2,128)}, u32[]{:S(2)}, u32[]{:S(2)}) %all-to-all-start) | async-done | bytes 819232 | tf_op jit(solution)/shard_map/all_to_all | solution.py:409
  68.4 0.0 copy-done
  68.4 8.7 %shard_map.41 = f32[1600,128]{1,0:T(8,128)} custom-call(s32[4,640]{1,0:T(4,128)S(1)} %pad.4.n_ref, f32[4,512]{1,0:T(4,128)S(1)} %get-tuple-element.17.s_ref, f32[1600,128]{1,0:T(8,128)} %bitcast.6.recv_ref, bf16[384,1024]{1,0:T(8,128)(2,1)S(1)} %copy-done, f32[20,80,128]{2,1,0:T(8,128)} %copy-done.2), custom_call_target="tpu_custom_call" | custom-call | flops 1258291200 | bytes 2443264 | tf_op jit(solution)/shard_map/pallas_call | solution.py:367
  77.1 5.6 %all-to-all-start.2 = ((f32[32,25,2,128]{3,2,1,0:T(2,128)}), f32[32,25,2,128]{3,2,1,0:T(2,128)S(1)}, u32[]{:S(2)}, u32[]{:S(2)}) async-start(f32[32,25,2,128]{3,2,1,0:T(2,128)} %bitcast.9), calls=%async_computation.2 | async-start | bytes 1638400 | tf_op jit(solution)/shard_map/all_to_all | solution.py:409
  82.7 5.5 %shard_map.42.b_ref = f32[20,80,128]{2,1,0:T(8,128)S(1)} custom-call(s32[4,640]{1,0:T(4,128)S(1)} %pad.4.n_ref, f32[4,512]{1,0:T(4,128)S(1)} %get-tuple-element.17.s_ref, f32[80,2560]{1,0:T(8,128)} %bitcast.23, bf16[384,1024]{1,0:T(8,128)(2,1)S(1)} %get-tuple-element.12.w_ref), custom_call_target="tpu_custom_call" | custom-call | flops 1258291200 | bytes 1624064 | tf_op jit(solution)/shard_map/pallas_call | solution.py:367
  88.2 16.0 %all-to-all-done.2 = f32[32,25,2,128]{3,2,1,0:T(2,128)S(1)} async-done(((f32[32,25,2,128]{3,2,1,0:T(2,128)}), f32[32,25,2,128]{3,2,1,0:T(2,128)S(1)}, u32[]{:S(2)}, u32[]{:S(2)}) %all-to-all-start.2) | async-done | bytes 819232 | tf_op jit(solution)/shard_map/all_to_all | solution.py:409
  104.3 2.0 %shard_map.43 = f32[80,2560]{1,0:T(8,128)} custom-call(f32[1600,128]{1,0:T(8,128)S(1)} %bitcast.18, f32[20,80,128]{2,1,0:T(8,128)S(1)} %shard_map.42.b_ref), custom_call_target="tpu_custom_call" | custom-call | flops 1048576 | bytes 1638400 | tf_op jit(solution)/shard_map/pallas_call | solution.py:367
  (9 shorter events, 0.1 us)
Async XLA Ops:
  0.0 17.9 %copy-start.4 = (s32[1,4,4,320]{3,2,1,0:T(4,128)S(1)}, s32[1,4,4,320]{3,2,1,0:T(4,128)}, u32[]{:S(2)}) copy-start(s32[1,4,4,320]{3,2,1,0:T(4,128)} %param.4) | copy-start | bytes 61444
  0.0 24.9 %collective-permute-start = (f32[80,2560]{1,0:T(8,128)}, f32[80,2560]{1,0:T(8,128)}, u32[]{:S(2)}, u32[]{:S(2)}) collective-permute-start(f32[80,2560]{1,0:T(8,128)} %bitcast.21), channel_id=1, source_target_pairs={{0,4},{1,5},{2,6},{3,7},{4,0},{5,1},{6,2},{7,3},{8,12},{9,13},{10,... | collective-permute-start | bytes 2457608 | tf_op jit(solution)/shard_map/ppermute | solution.py:412
  6.2 34.6 %all-to-all-start.1 = ((f32[32,25,2,128]{3,2,1,0:T(2,128)}), f32[32,25,2,128]{3,2,1,0:T(2,128)S(1)}, u32[]{:S(2)}, u32[]{:S(2)}) async-start(f32[32,25,2,128]{3,2,1,0:T(2,128)} %bitcast.19), calls=%async_computation.1 | async-start | bytes 1638400 | tf_op jit(solution)/shard_map/all_to_all | solution.py:409
  24.9 1.1 %copy-start.1 = (bf16[384,1024]{1,0:T(8,128)(2,1)S(1)}, bf16[384,1024]{1,0:T(8,128)(2,1)}, u32[]{:S(2)}) copy-start(bf16[384,1024]{1,0:T(8,128)(2,1)} %get-tuple-element.9.w_ref) | copy-start | bytes 2359300
  40.8 5.6 %copy-start.3 = (f32[32,25,2,128]{3,2,1,0:T(2,128)}, f32[32,25,2,128]{3,2,1,0:T(2,128)S(1)}, u32[]{:S(2)}) copy-start(f32[32,25,2,128]{3,2,1,0:T(2,128)S(1)} %all-to-all-done.1) | copy-start | bytes 2457604
  40.8 27.7 %all-to-all-start = ((f32[32,25,2,128]{3,2,1,0:T(2,128)}), f32[32,25,2,128]{3,2,1,0:T(2,128)}, u32[]{:S(2)}, u32[]{:S(2)}) async-start(f32[32,25,2,128]{3,2,1,0:T(2,128)} %bitcast.5), calls=%async_computation | async-start | bytes 1638400 | tf_op jit(solution)/shard_map/all_to_all | solution.py:409
  46.4 22.0 %copy-start = (bf16[384,1024]{1,0:T(8,128)(2,1)S(1)}, bf16[384,1024]{1,0:T(8,128)(2,1)}, u32[]{:S(2)}) copy-start(bf16[384,1024]{1,0:T(8,128)(2,1)} %get-tuple-element.10.w_ref) | copy-start | bytes 2359300
  52.9 0.9 copy-start.2
  77.1 27.2 %all-to-all-start.2 = ((f32[32,25,2,128]{3,2,1,0:T(2,128)}), f32[32,25,2,128]{3,2,1,0:T(2,128)S(1)}, u32[]{:S(2)}, u32[]{:S(2)}) async-start(f32[32,25,2,128]{3,2,1,0:T(2,128)} %bitcast.9), calls=%async_computation.2 | async-start | bytes 1638400 | tf_op jit(solution)/shard_map/all_to_all | solution.py:409

commit v6 on v5

--- a/solution.py
+++ b/solution.py
@@ -432,8 +432,8 @@
         pl.ANY,
     )
     cross_in = exchange(mixed)
-    beta = call(beta_kernel, summed, work, (*lists, own, w0), flops, (2,))
-    alpha = call(alpha_kernel, summed, [*work, pieces], (*lists, columns_in, w1), flops, (2,))
+    beta = call(beta_kernel, summed, work, (*lists, own, w0), flops, (2,), room=52)
+    alpha = call(alpha_kernel, summed, [*work, pieces], (*lists, columns_in, w1), flops, (2,), room=51)
     cross = call(
         cross_kernel,
         packed,
@@ -441,6 +441,7 @@
         (*lists, cross_in, w2, alpha),
         flops,
         (2,),
+        room=51,
     )
     returned = exchange(cross)
     out = call(

time: 107 us -> 106 us (level)
  Pallas kernels: 38 us -> 35.7 us
  local copies, waits for them, and re-layouts: 2.34 us -> 4.38 us
    pallas_call x7, Pallas kernels: 38 us -> 35.7 us  [call(): pl.pallas_call(kernel, out_shape=out, in_specs=specs, out_specs=jax.tree....]
    unnamed x12 -> x16, local copies, waits for them, and re-layouts: 2.13 us -> 4.18 us
  transfers between devices with their start and end apart: 4 -> 4, of which waited for: 3 -> 3; matrix products, arithmetic and copies ran while one was open for 2% -> 2% of each run, Pallas kernels for 26% -> 25%
where the time goes in v6:
time: 106 us; the launch traced here: 105 us
  waiting for transfers between devices  37 us (35%)
  Pallas kernels  35.7 us (34%)
  starting transfers between devices  25.9 us (24%)
  local copies, waits for them, and re-layouts  4.38 us (4%)
  other arithmetic  1.96 us (2%)
    all_to_all x3, waiting for transfers between devices, exchange(): x = lax.all_to_all(x, 'rows', split_axis=0, concat_axis=0, tiled=True)  37 us
    pallas_call x7, Pallas kernels, call(): pl.pallas_call(kernel, out_shape=out, in_specs=specs, out_specs=jax.tree....  35.7 us
    all_to_all x3, starting transfers between devices, exchange(): x = lax.all_to_all(x, 'rows', split_axis=0, concat_axis=0, tiled=True)  22.9 us
    unnamed x16, local copies, waits for them, and re-layouts  4.18 us
    ppermute x1, starting transfers between devices, steps(): lax.ppermute(own, 'irrep', [(i, i ^ irreps // 2) for i in range(irreps)])  3.02 us
  transfers between devices with their start and end apart: 4, of which 3 were waited for; matrix products, arithmetic and copies ran while one was open for 2% of the time, Pallas kernels for 25%

profile of v6, /device:TPU:8, one launch (start us, length us, event | category | flops | bytes accessed | tf_op | source)
XLA Modules:
  0.0 105.1 jit_solution(12140102433235442358)
XLA Ops:
  0.0 3.0 %collective-permute-start = (f32[80,2560]{1,0:T(8,128)}, f32[80,2560]{1,0:T(8,128)S(1)}, u32[]{:S(2)}, u32[]{:S(2)}) collective-permute-start(f32[80,2560]{1,0:T(8,128)} %bitcast.23), channel_id=1, source_target_pairs={{0,4},{1,5},{2,6},{3,7},{4,0},{5,1},{6,2},{7,3},{8,12},{9,13},{10,... | collective-permute-start | bytes 2457608 | tf_op jit(solution)/shard_map/ppermute | solution.py:412
  3.0 3.1 %shard_map.39 = f32[1600,128]{1,0:T(8,128)} custom-call(f32[80,2560]{1,0:T(8,128)} %bitcast.24), custom_call_target="tpu_custom_call" | custom-call | flops 1048576 | bytes 819200 | tf_op jit(solution)/shard_map/pallas_call | solution.py:367
  6.2 11.7 %all-to-all-start.1 = ((f32[32,25,2,128]{3,2,1,0:T(2,128)}), f32[32,25,2,128]{3,2,1,0:T(2,128)S(1)}, u32[]{:S(2)}, u32[]{:S(2)}) async-start(f32[32,25,2,128]{3,2,1,0:T(2,128)} %bitcast.21), calls=%async_computation.1 | async-start | bytes 1638400 | tf_op jit(solution)/shard_map/all_to_all | solution.py:409
  17.9 0.0 copy-done.5
  18.0 0.4 convert_reduce_fusion.1
  18.5 0.1 select_reduce_fusion.1
  18.6 0.7 convert_reduce_fusion
  19.3 0.5 select_reduce_fusion
  19.9 0.1 rem.42
  20.0 0.1 copy.19
  20.1 0.1 copy.15
  20.2 0.1 pad_add_fusion
  20.2 4.7 %shard_map.37 = (bf16[384,1024]{1,0:T(8,128)(2,1)S(1)}, bf16[384,1024]{1,0:T(8,128)(2,1)S(1)}, bf16[384,1024]{1,0:T(8,128)(2,1)}, bf16[384,1024]{1,0:T(8,128)(2,1)}) custom-call(f32[4,8,128,128]{3,2,1,0:T(8,128)} %bitcast.22), custom_call_target="tpu_custom_call" | custom-call | flops 1048576 | bytes 2097152 | tf_op jit(solution)/shard_map/pallas_call | solution.py:367
  24.9 0.0 collective-permute-done.c_ref
  24.9 0.9 copy-done.6
  25.9 1.1 %copy-done.3 = bf16[384,1024]{1,0:T(8,128)(2,1)S(1)} copy-done((bf16[384,1024]{1,0:T(8,128)(2,1)S(1)}, bf16[384,1024]{1,0:T(8,128)(2,1)}, u32[]{:S(2)}) %copy-start.3) | copy-done | bytes 786456
  27.0 7.5 %shard_map.38 = f32[1600,128]{1,0:T(8,128)} custom-call(s32[4,640]{1,0:T(4,128)S(1)} %pad.4.n_ref, f32[4,512]{1,0:T(4,128)S(1)} %get-tuple-element.17.s_ref, f32[80,2560]{1,0:T(8,128)} %copy-done.6, bf16[384,1024]{1,0:T(8,128)(2,1)S(1)} %copy-done.3), custom_call_target="tpu_custom_call" | custom-call | flops 1258291200 | bytes 1624064 | tf_op jit(solution)/shard_map/pallas_call | solution.py:367
  34.5 0.0 copy-done.1
  34.5 6.2 %all-to-all-done.1 = f32[32,25,2,128]{3,2,1,0:T(2,128)S(1)} async-done(((f32[32,25,2,128]{3,2,1,0:T(2,128)}), f32[32,25,2,128]{3,2,1,0:T(2,128)S(1)}, u32[]{:S(2)}, u32[]{:S(2)}) %all-to-all-start.1) | async-done | bytes 819232 | tf_op jit(solution)/shard_map/all_to_all | solution.py:409
  40.8 5.6 %all-to-all-start = ((f32[32,25,2,128]{3,2,1,0:T(2,128)}), f32[32,25,2,128]{3,2,1,0:T(2,128)S(1)}, u32[]{:S(2)}, u32[]{:S(2)}) async-start(f32[32,25,2,128]{3,2,1,0:T(2,128)} %bitcast.5), calls=%async_computation | async-start | bytes 1638400 | tf_op jit(solution)/shard_map/all_to_all | solution.py:409
  46.3 0.0 copy-start.2
  46.4 1.1 %copy-done.2 = bf16[384,1024]{1,0:T(8,128)(2,1)S(1)} copy-done((bf16[384,1024]{1,0:T(8,128)(2,1)S(1)}, bf16[384,1024]{1,0:T(8,128)(2,1)}, u32[]{:S(2)}) %copy-start.2) | copy-done | bytes 786456
  47.5 5.2 %shard_map.40.alpha_ref = f32[20,80,128]{2,1,0:T(8,128)S(1)} custom-call(s32[4,640]{1,0:T(4,128)S(1)} %pad.4.n_ref, f32[4,512]{1,0:T(4,128)S(1)} %get-tuple-element.17.s_ref, f32[1600,128]{1,0:T(8,128)S(1)} %bitcast.19, bf16[384,1024]{1,0:T(8,128)(2,1)S(1)} %copy-done.2), custom_call_target="tpu_custom_call" | custom-call | flops 1258291200 | bytes 1624064 | tf_op jit(solution)/shard_map/pallas_call | solution.py:367
  52.7 0.0 copy-start.4
  52.7 0.9 copy-done.4
  53.6 14.7 %all-to-all-done = f32[32,25,2,128]{3,2,1,0:T(2,128)S(1)} async-done(((f32[32,25,2,128]{3,2,1,0:T(2,128)}), f32[32,25,2,128]{3,2,1,0:T(2,128)S(1)}, u32[]{:S(2)}, u32[]{:S(2)}) %all-to-all-start) | async-done | bytes 819232 | tf_op jit(solution)/shard_map/all_to_all | solution.py:409
  68.3 0.0 copy-done
  68.3 7.5 %shard_map.41 = f32[1600,128]{1,0:T(8,128)} custom-call(s32[4,640]{1,0:T(4,128)S(1)} %pad.4.n_ref, f32[4,512]{1,0:T(4,128)S(1)} %get-tuple-element.17.s_ref, f32[1600,128]{1,0:T(8,128)S(1)} %bitcast.20, bf16[384,1024]{1,0:T(8,128)(2,1)S(1)} %copy-done, f32[20,80,128]{2,1,0:T(8,128)} %copy-done.4), custom_call_target="tpu_custom_call" | custom-call | flops 1258291200 | bytes 2443264 | tf_op jit(solution)/shard_map/pallas_call | solution.py:367
  75.9 5.6 %all-to-all-start.2 = ((f32[32,25,2,128]{3,2,1,0:T(2,128)}), f32[32,25,2,128]{3,2,1,0:T(2,128)S(1)}, u32[]{:S(2)}, u32[]{:S(2)}) async-start(f32[32,25,2,128]{3,2,1,0:T(2,128)} %bitcast.9), calls=%async_computation.2 | async-start | bytes 1638400 | tf_op jit(solution)/shard_map/all_to_all | solution.py:409
  81.5 5.5 %shard_map.42.b_ref = f32[20,80,128]{2,1,0:T(8,128)S(1)} custom-call(s32[4,640]{1,0:T(4,128)S(1)} %pad.4.n_ref, f32[4,512]{1,0:T(4,128)S(1)} %get-tuple-element.17.s_ref, f32[80,2560]{1,0:T(8,128)} %bitcast.25, bf16[384,1024]{1,0:T(8,128)(2,1)S(1)} %get-tuple-element.12.w_ref), custom_call_target="tpu_custom_call" | custom-call | flops 1258291200 | bytes 1624064 | tf_op jit(solution)/shard_map/pallas_call | solution.py:367
  87.0 16.1 %all-to-all-done.2 = f32[32,25,2,128]{3,2,1,0:T(2,128)S(1)} async-done(((f32[32,25,2,128]{3,2,1,0:T(2,128)}), f32[32,25,2,128]{3,2,1,0:T(2,128)S(1)}, u32[]{:S(2)}, u32[]{:S(2)}) %all-to-all-start.2) | async-done | bytes 819232 | tf_op jit(solution)/shard_map/all_to_all | solution.py:409
  103.1 2.0 %shard_map.43 = f32[80,2560]{1,0:T(8,128)} custom-call(f32[1600,128]{1,0:T(8,128)S(1)} %bitcast.18, f32[20,80,128]{2,1,0:T(8,128)S(1)} %shard_map.42.b_ref), custom_call_target="tpu_custom_call" | custom-call | flops 1048576 | bytes 1638400 | tf_op jit(solution)/shard_map/pallas_call | solution.py:367
  (13 shorter events, 0.1 us)
Async XLA Ops:
  0.0 17.9 %copy-start.5 = (s32[1,4,4,320]{3,2,1,0:T(4,128)S(1)}, s32[1,4,4,320]{3,2,1,0:T(4,128)}, u32[]{:S(2)}) copy-start(s32[1,4,4,320]{3,2,1,0:T(4,128)} %param.4) | copy-start | bytes 61444
  0.0 24.9 %collective-permute-start = (f32[80,2560]{1,0:T(8,128)}, f32[80,2560]{1,0:T(8,128)S(1)}, u32[]{:S(2)}, u32[]{:S(2)}) collective-permute-start(f32[80,2560]{1,0:T(8,128)} %bitcast.23), channel_id=1, source_target_pairs={{0,4},{1,5},{2,6},{3,7},{4,0},{5,1},{6,2},{7,3},{8,12},{9,13},{10,... | collective-permute-start | bytes 2457608 | tf_op jit(solution)/shard_map/ppermute | solution.py:412
  6.2 34.6 %all-to-all-start.1 = ((f32[32,25,2,128]{3,2,1,0:T(2,128)}), f32[32,25,2,128]{3,2,1,0:T(2,128)S(1)}, u32[]{:S(2)}, u32[]{:S(2)}) async-start(f32[32,25,2,128]{3,2,1,0:T(2,128)} %bitcast.21), calls=%async_computation.1 | async-start | bytes 1638400 | tf_op jit(solution)/shard_map/all_to_all | solution.py:409
  24.9 9.6 %copy-start.1 = (bf16[384,1024]{1,0:T(8,128)(2,1)}, bf16[384,1024]{1,0:T(8,128)(2,1)S(1)}, u32[]{:S(2)}) copy-start(bf16[384,1024]{1,0:T(8,128)(2,1)S(1)} %get-tuple-element.11.w_ref) | copy-start | bytes 2359300
  24.9 0.9 copy-start.6
  25.9 1.1 %copy-start.3 = (bf16[384,1024]{1,0:T(8,128)(2,1)S(1)}, bf16[384,1024]{1,0:T(8,128)(2,1)}, u32[]{:S(2)}) copy-start(bf16[384,1024]{1,0:T(8,128)(2,1)} %get-tuple-element.9.w_ref) | copy-start | bytes 2359300
  40.8 27.6 %all-to-all-start = ((f32[32,25,2,128]{3,2,1,0:T(2,128)}), f32[32,25,2,128]{3,2,1,0:T(2,128)S(1)}, u32[]{:S(2)}, u32[]{:S(2)}) async-start(f32[32,25,2,128]{3,2,1,0:T(2,128)} %bitcast.5), calls=%async_computation | async-start | bytes 1638400 | tf_op jit(solution)/shard_map/all_to_all | solution.py:409
  46.3 1.1 %copy-start.2 = (bf16[384,1024]{1,0:T(8,128)(2,1)S(1)}, bf16[384,1024]{1,0:T(8,128)(2,1)}, u32[]{:S(2)}) copy-start(bf16[384,1024]{1,0:T(8,128)(2,1)} %copy-done.1) | copy-start | bytes 2359300
  47.5 20.9 %copy-start = (bf16[384,1024]{1,0:T(8,128)(2,1)S(1)}, bf16[384,1024]{1,0:T(8,128)(2,1)}, u32[]{:S(2)}) copy-start(bf16[384,1024]{1,0:T(8,128)(2,1)} %get-tuple-element.10.w_ref) | copy-start | bytes 2359300
  52.7 0.9 copy-start.4
  75.9 27.2 %all-to-all-start.2 = ((f32[32,25,2,128]{3,2,1,0:T(2,128)}), f32[32,25,2,128]{3,2,1,0:T(2,128)S(1)}, u32[]{:S(2)}, u32[]{:S(2)}) async-start(f32[32,25,2,128]{3,2,1,0:T(2,128)} %bitcast.9), calls=%async_computation.2 | async-start | bytes 1638400 | tf_op jit(solution)/shard_map/all_to_all | solution.py:409
